TPU v7x, 32 devices: a whole 2x2x4 slice. The times are simulated.
32 devices in a mesh: elem: 8 (over y, x, core), mode: 4 (over z).
Axes of the slice: x: 2, y: 2, z: 4, core: 2. Of those that a mesh axis runs over, the one named last changes fastest.
Arguments:
- velocity: float32 [3, 5184, 2, 512], P(None, 'elem', None, 'mode'), may hold values from -3 to 3
- column_width: float32 [8], P('elem'), may hold values from 0.5 to 2
- row_height: float32 [8], replicated, may hold values from 0.5 to 2
- disc_mask: int32 [64], P('elem'), may hold values from 0 to 1, as said below
Outputs:
- velocity_new: float32 [3, 5184, 2, 512], P(None, 'elem', None, 'mode')
Inputs may be any that keep to these rules, and one draw needn't show every extreme that they name: `disc_mask`: in each column of 8 elements the ones form one run of 2 to 4 consecutive rows, counted cyclically in y.
All inputs are finite; a program needn't handle non-finite values.
Results may differ from a plain program's by a relative error of at most 0.0001.
Values sent between devices are 32-bit elements; how exact they have to be, the bound alone decides.
A program may use at most 128 MiB of HBM per device.

v0:
```python
import math

import jax
import jax.numpy as jnp
import numpy as np
from jax import lax
from jax.sharding import PartitionSpec as P

ORDER = 8
ITERS = 2


gll_points = [
    -1.0,
    -0.8997579954114602,
    -0.6771862795107377,
    -0.3631174638261782,
    0.0,
    0.3631174638261782,
    0.6771862795107377,
    0.8997579954114602,
    1.0,
]
gll_weights = [
    0.0277777777777778,
    0.1654953615608055,
    0.2745387125001617,
    0.3464285109730463,
    0.3715192743764172,
    0.3464285109730463,
    0.2745387125001617,
    0.1654953615608055,
    0.0277777777777778,
]
viscosity = 0.5
time_step = 0.02
thrust_coef = 4.0 / 3.0
highest = lax.Precision.HIGHEST


def padded(shard, sides, width):
    for axis, dim in sides:
        peers, length = (lax.axis_size(axis), shard.shape[dim])
        up = [(i, (i + 1) % peers) for i in range(peers)]
        down = [(j, i) for i, j in up]
        last = lax.slice_in_dim(shard, length - width, length, axis=dim)
        initial = lax.slice_in_dim(shard, 0, width, axis=dim)
        before = lax.ppermute(last, axis, up)
        after = lax.ppermute(initial, axis, down)
        shard = jnp.concatenate([before, shard, after], axis=dim)
    return shard


def node_tables():
    points = np.array(gll_points)
    identity = np.eye(9)
    differences = points[:, None] - points[None, :] + identity
    barycentric = 1.0 / np.prod(differences, axis=1)
    off_diagonal = barycentric[None, :] / barycentric[:, None] / differences * (1.0 - identity)
    derivative = off_diagonal - identity * off_diagonal.sum(axis=1)[:, None]
    return (
        jnp.asarray(derivative, dtype=jnp.float32),
        jnp.asarray(np.array(gll_weights), dtype=jnp.float32),
    )


def spectral_tables(mode_count):
    planes = 3 * mode_count
    wave_index = jnp.arange(mode_count, dtype=jnp.int32)
    plane_index = jnp.arange(planes, dtype=jnp.int32)
    phase_index = wave_index[:, None] * plane_index[None, :] % planes
    angles = 2.0 * math.pi / planes * phase_index.astype(jnp.float32)
    cosine_table = jnp.cos(angles)
    sine_table = jnp.sin(angles)
    mode_weight = jnp.where(wave_index == 0, 1.0, 2.0).astype(jnp.float32)[:, None] / math.sqrt(
        mode_count
    )
    wave_number = 8.0 / mode_count * wave_index.astype(jnp.float32)[:, None]
    inverse = jnp.concatenate([mode_weight * cosine_table, -mode_weight * sine_table], axis=0)
    spanwise = jnp.concatenate(
        [-wave_number * mode_weight * sine_table, -wave_number * mode_weight * cosine_table], axis=0
    )
    forward = (
        math.sqrt(mode_count) / planes * jnp.concatenate([cosine_table, -sine_table], axis=0).T
    )
    return (inverse, spanwise, forward)


def assemble(nodal_field):
    extended = padded(nodal_field, (("elem", 2),), 1)
    first_layer = nodal_field[:, :, 0] + extended[:, :, 0]
    last_layer = nodal_field[:, :, 8] + extended[:, :, 10]
    nodal_field = jnp.concatenate(
        [first_layer[:, :, None], nodal_field[:, :, 1:8], last_layer[:, :, None]], axis=2
    )
    upper_layer = nodal_field[:, :, :, 8] + jnp.roll(nodal_field[:, :, :, 0], -1, axis=1)
    return jnp.concatenate(
        [
            jnp.roll(upper_layer, 1, axis=1)[:, :, :, None],
            nodal_field[:, :, :, 1:8],
            upper_layer[:, :, :, None],
        ],
        axis=3,
    )


def apply_operator(nodal_field, derivative, quad_weights, ratio_x, ratio_y, jacobian, factor):
    grad_r = jnp.einsum("ij,pejbl->peibl", derivative, nodal_field, precision=highest)
    grad_s = jnp.einsum("ij,peajl->peail", derivative, nodal_field, precision=highest)
    flux_r = grad_r * quad_weights[None, None, :, :, None] * ratio_x[None, :, None, None, None]
    flux_s = grad_s * quad_weights[None, None, :, :, None] * ratio_y[None, :, None, None, None]
    stiffness = jnp.einsum("ji,pejbl->peibl", derivative, flux_r, precision=highest) + jnp.einsum(
        "ji,peajl->peail", derivative, flux_s, precision=highest
    )
    masses = (
        jacobian[None, :, None, None, None] * quad_weights[None, None, :, :, None] * nodal_field
    )
    return assemble(factor * masses + viscosity * stiffness)


def weighted_sum(left_field, right_field, multiplicity):
    return jnp.sum(left_field * right_field * multiplicity[None, None, :, :, None], axis=(1, 2, 3))


def paired(residual, image_field, multiplicity):
    return lax.psum(
        (
            weighted_sum(residual, residual, multiplicity),
            weighted_sum(residual, image_field, multiplicity),
        ),
        "elem",
    )


def on_device(velocity, column_width, row_height, disc_mask):
    derivative, weights = node_tables()
    quad_weights = weights[:, None] * weights[None, :]
    node_index = jnp.arange(9)
    edge_count = jnp.where((node_index == 0) | (node_index == 8), 2.0, 1.0).astype(jnp.float32)
    multiplicity = 1.0 / (edge_count[:, None] * edge_count[None, :])
    groups = lax.axis_size("mode")
    local_modes = velocity.shape[3]
    mode_count = groups * local_modes
    planes = 3 * mode_count
    elements = velocity.shape[1] // 81
    local_elems = elements // groups
    col_width = column_width[0]
    inverse, spanwise, forward = spectral_tables(mode_count)
    nodal_field = velocity.reshape(3, elements, 9, 9, 2 * local_modes)
    mode_index = lax.axis_index("mode") * local_modes + jnp.arange(local_modes, dtype=jnp.int32)
    wavenumber = 8.0 / mode_count * mode_index.astype(jnp.float32)
    elem_start = lax.axis_index("mode") * local_elems
    local_heights = lax.dynamic_slice_in_dim(row_height, elem_start, local_elems)
    local_disc = lax.dynamic_slice_in_dim(disc_mask, elem_start, local_elems).astype(jnp.float32)
    members = lax.all_to_all(velocity, "mode", split_axis=1, concat_axis=3, tiled=True)
    flat_items = members.reshape(members.shape[0], members.shape[1], 2 * mode_count)
    values = jnp.einsum("pnl,lq->pnq", flat_items, inverse, precision=highest)
    along_z = jnp.einsum("pnl,lq->pnq", flat_items, spanwise, precision=highest)
    values = values.reshape(3, local_elems, 9, 9, planes)
    along_z = along_z.reshape(3, local_elems, 9, 9, planes)
    along_x = 2.0 / col_width * jnp.einsum("ij,pejbq->peibq", derivative, values, precision=highest)
    along_y = (2.0 / local_heights)[None, :, None, None, None] * jnp.einsum(
        "ij,peajq->peaiq", derivative, values, precision=highest
    )
    advection = values[0][None] * along_x + values[1][None] * along_y + values[2][None] * along_z
    plane_index = jnp.arange(planes)
    in_disc = ((plane_index >= 3 * planes // 8) & (plane_index < 5 * planes // 8)).astype(
        jnp.float32
    )
    disc_planes = 5 * planes // 8 - 3 * planes // 8
    local_jacobian = col_width * local_heights / 4.0
    node_weight = (local_disc * local_jacobian)[:, None, None] * quad_weights[None]
    partial_total = jnp.sum(node_weight[:, :, :, None] * values[0] * values[0] * in_disc)
    disc_total = lax.psum(partial_total, "mode")
    disc_area = disc_planes * col_width * jnp.sum(disc_mask.astype(jnp.float32) * row_height)
    pressure = disc_total / disc_area
    thrust = (
        -(0.5 * thrust_coef * ORDER)
        * pressure
        / col_width
        * local_disc[:, None, None, None]
        * in_disc
    )
    tendency = jnp.concatenate([(thrust - advection[0])[None], -advection[1:]], axis=0)
    spectral = jnp.einsum("peabq,ql->peabl", tendency, forward, precision=highest)
    spectral = spectral.reshape(3, local_elems * 81, 2, mode_count)
    returned = lax.all_to_all(spectral, "mode", split_axis=3, concat_axis=1, tiled=True)
    u_star = nodal_field + time_step * returned.reshape(3, elements, 9, 9, 2 * local_modes)
    jacobian = col_width * row_height / 4.0
    ratio_x = row_height / col_width
    ratio_y = col_width / row_height
    single = 1.0 / time_step + viscosity * wavenumber * wavenumber
    factor = jnp.concatenate([single, single])
    right_side = (
        assemble(
            jacobian[None, :, None, None, None] * quad_weights[None, None, :, :, None] * u_star
        )
        / time_step
    )
    residual = right_side
    solution = jnp.zeros_like(right_side)
    image_field = apply_operator(
        residual, derivative, quad_weights, ratio_x, ratio_y, jacobian, factor
    )
    norm_now, product = paired(residual, image_field, multiplicity)
    step_size = norm_now / product
    direction = residual
    along_image = image_field
    for iteration in range(ITERS):
        solution = solution + step_size[:, None, None, None, :] * direction
        residual = residual - step_size[:, None, None, None, :] * along_image
        if iteration + 1 < ITERS:
            image_field = apply_operator(
                residual, derivative, quad_weights, ratio_x, ratio_y, jacobian, factor
            )
            norm_next, product = paired(residual, image_field, multiplicity)
            beta_ratio = norm_next / norm_now
            step_size = norm_next / (product - beta_ratio * norm_next / step_size)
            direction = residual + beta_ratio[:, None, None, None, :] * direction
            along_image = image_field + beta_ratio[:, None, None, None, :] * along_image
            norm_now = norm_next
    return solution.reshape(3, elements * 81, 2, local_modes)


def solution(mesh):
    return jax.shard_map(
        on_device,
        mesh=mesh,
        in_specs=(P(None, "elem", None, "mode"), P("elem"), P(), P("elem")),
        out_specs=P(None, "elem", None, "mode"),
        check_vma=False,
    )
```

profile of v0, /device:TPU:0, one launch (start us, length us, event | category | flops | bytes accessed | tf_op | source)
XLA Modules:
  0.0 403.9 jit_solution(6718678095885858187)
XLA Ops:
  0.0 3.6 copy.119
  3.6 6.3 %all-to-all-start = ((f32[3,648,2,128]{3,2,0,1:T(2,128)}), f32[3,648,2,128]{3,2,0,1:T(2,128)S(1)}, u32[]{:S(2)}, u32[]{:S(2)}) async-start(f32[3,648,2,128]{3,2,0,1:T(2,128)} %copy.119), calls=%async_computation | async-start | bytes 3981312 | tf_op jit(solution)/shard_map/all_to_all | solution.py:155
  13.6 14.0 %fusion.61 = (f32[512,1536]{1,0:T(8,128)}, f32[512,1536]{1,0:T(8,128)}) fusion(), kind=kLoop, calls=%fused_computation.87 | loop fusion | flops 7864320 | bytes 6291456 | tf_op jit(solution)/shard_map/cos | solution.py:73
  27.5 14.2 %fusion.63 = (f32[512,1536]{1,0:T(8,128)}, f32[512,1536]{1,0:T(8,128)}) fusion(f32[512]{0:T(512)S(1)} %negate_multiply_fusion), kind=kLoop, calls=%fused_computation.89 | loop fusion | flops 8650752 | bytes 6293504 | tf_op jit(solution)/shard_map/mul | solution.py:81
  41.7 14.2 %fusion.64 = (f32[512,1536]{1,0:T(8,128)}, f32[512,1536]{1,0:T(8,128)}) fusion(f32[512]{0:T(512)S(1)} %fusion.77, f32[512]{0:T(512)S(1)} %select_multiply_fusion), kind=kLoop, calls=%fused_computation.90 | loop fusion | flops 8650752 | bytes 6295552 | tf_op jit(solution)/shard_map/mul | solution.py:79
  57.7 3.6 reshape.205
  61.3 13.4 %fusion.54 = f32[3,162,1536]{2,1,0:T(8,128)S(1)} fusion(f32[3,162,1024]{2,1,0:T(8,128)} %reshape.205, f32[512,1536]{1,0:T(8,128)S(1)} %copy-done.11, f32[512,1536]{1,0:T(8,128)} %get-tuple-element.64), kind=kOutput, calls=%fused_computation.79 | convolution fusion | flops 9174515712 | bytes 11268096 | tf_op jit(solution)/shard_map/pnl,lq->pnq/dot_general | solution.py:157
  74.7 4.0 copy.122
  79.1 2.4 fusion.74
  82.3 2.5 mul.635
  86.9 2.5 mul.641
  89.5 3.5 copy.127
  92.9 13.4 %fusion.53 = f32[3,162,1536]{2,1,0:T(8,128)S(1)} fusion(f32[3,162,1024]{2,1,0:T(8,128)} %reshape.205, f32[512,1536]{1,0:T(8,128)} %get-tuple-element.56, f32[512,1536]{1,0:T(8,128)S(1)} %copy-done.10), kind=kOutput, calls=%fused_computation.78 | convolution fusion | flops 9174515712 | bytes 11268096 | tf_op jit(solution)/shard_map/pnl,lq->pnq/dot_general | solution.py:158
  106.4 4.2 %copy.128 = f32[3,162,1536]{2,0,1:T(4,128)} copy(f32[3,162,1536]{2,1,0:T(8,128)S(1)} %fusion.53) | data formatting | bytes 5971968 | tf_op jit(solution)/shard_map/pnl,lq->pnq/dot_general | solution.py:158
  110.6 12.8 %psum.35 = f32[]{:T(128)} all-reduce(f32[]{:T(128)} %get-tuple-element.35), channel_id=1, replica_groups=mesh['elem'=8,'mode'=4] {'mode'}, use_global_device_ids=true, to_apply=%region_1.2 | all-reduce | flops 1 | bytes 8 | tf_op jit(solution)/shard_map/psum | solution.py:174
  125.6 11.5 %fusion.16 = f32[3,2,9,1536,9]{3,4,2,1,0:T(8,128)} fusion(f32[9,9,1,1,1]{1,0,4,3,2:T(8,128)S(1)} %copy-done.13, f32[3,2,9,9,1536]{4,0,3,2,1:T(4,128)} %bitcast.137), kind=kOutput, calls=%fused_computation.24 | convolution fusion | flops 80621568 | bytes 5972292 | tf_op jit(solution)/shard_map/ij,peajq->peaiq/dot_general | solution.py:162
  137.1 14.2 %fusion.15 = f32[3,2,9,9,1536]{4,2,3,1,0:T(8,128)S(1)} fusion(f32[3,2,9,9,1536]{4,0,3,2,1:T(4,128)S(1)} %bitcast.139, f32[3,2,9,1536,9]{3,4,2,1,0:T(8,128)} %fusion.16, f32[9,9,1,1,1]{1,0,4,3,2:T(8,128)S(1)} %copy-done.13, f32[3,2,9,9,1536]{4,0,3,2,1:T(4,128)S(1)} %bitcast.138, f32[2,9,9,1536]{3,1,2,0:T(8,128)S(1)} %copy-done.3, f32[2]{0:T(128)S(1)} %copy-done.30, ...), kind=kOutput, calls=%fused_computation.20 | convolution fusion | flops 85847040 | bytes 14930256 | tf_op jit(solution)/shard_map/ij,pejbq->peibq/dot_general | solution.py:161
  154.3 17.1 %fusion.7 = f32[3,2,9,9,1024]{4,2,3,1,0:T(8,128)S(1)} fusion(f32[512,1536]{1,0:T(8,128)S(1)} %copy-done.9, f32[512,1536]{1,0:T(8,128)S(1)} %copy-done.8, f32[2,2,9,9,1536]{4,2,3,1,0:T(8,128)S(1)} %slice_negate_fusion, f32[1,2,9,9,1536]{4,2,3,1,0:T(8,128)S(1)} %slice_subtract_fusion), kind=kOutput, calls=%fused_computation.10 | convolution fusion | flops 9176835072 | bytes 11268096 | tf_op jit(solution)/shard_map/peabq,ql->peabl/dot_general | solution.py:185
  172.8 3.1 reshape.208
  176.0 6.6 %copy.132 = f32[3,162,2,512]{1,2,0,3:T(2,128)} copy(f32[3,162,2,512]{3,2,0,1:T(2,128)} %reshape.208) | data formatting | bytes 3981312 | tf_op jit(solution)/shard_map/reshape | solution.py:186
  182.5 4.7 %all-to-all-start.1 = ((f32[3,162,2,512]{1,2,0,3:T(2,128)}), f32[3,162,2,512]{1,2,0,3:T(2,128)}, u32[]{:S(2)}, u32[]{:S(2)}) async-start(f32[3,162,2,512]{1,2,0,3:T(2,128)} %copy.132), calls=%async_computation.1 | async-start | bytes 6291456 | tf_op jit(solution)/shard_map/all_to_all | solution.py:187
  187.2 3.2 reshape.217
  192.3 63.4 %all-to-all-done.1 = f32[3,162,2,512]{1,2,0,3:T(2,128)} async-done(((f32[3,162,2,512]{1,2,0,3:T(2,128)}), f32[3,162,2,512]{1,2,0,3:T(2,128)}, u32[]{:S(2)}, u32[]{:S(2)}) %all-to-all-start.1) | async-done | bytes 1990688 | tf_op jit(solution)/shard_map/all_to_all | solution.py:187
  255.6 5.2 %broadcast_multiply_fusion = f32[3,162,2,512]{1,2,0,3:T(2,128)} fusion(f32[3,162,2,512]{1,2,0,3:T(2,128)} %all-to-all-done.1), kind=kLoop, calls=%fused_computation.101 | loop fusion | flops 497664 | bytes 3981312 | tf_op jit(solution)/shard_map/mul | solution.py:188
  260.8 6.4 %copy.133 = f32[3,162,2,4,128]{4,2,0,1,3:T(2,128)} copy(f32[3,162,2,4,128]{1,2,0,4,3:T(2,128)} %bitcast.140) | data formatting | bytes 3981312 | tf_op jit(solution)/shard_map/mul | solution.py:188
  267.2 4.7 %mul.655 = f32[3,8,9,9,256]{4,0,3,2,1:T(4,128)} reshape(f32[3,4,162,2,128]{4,3,0,2,1:T(2,128)} %bitcast.143) | data formatting | bytes 3981312 | tf_op jit(solution)/shard_map/mul | solution.py:188
  271.9 3.3 fusion.36
  275.6 2.6 collective-permute-start.1
  278.5 3.9 collective-permute-done
  285.0 4.9 %fusion.44 = f32[3,8,9,256,9]{3,4,2,1,0:T(8,128)S(1)} fusion(f32[9,9,1,1,1]{1,0,4,3,2:T(8,128)S(1)} %copy-done.13, f32[3,8,9,9,256]{4,2,3,1,0:T(8,128)S(1)} %copy_multiply_fusion.4), kind=kOutput, calls=%fused_computation.64 | convolution fusion | flops 53747712 | bytes 3981636 | tf_op jit(solution)/shard_map/ij,peajl->peail/dot_general | solution.py:109
  290.0 4.2 %fusion.33 = f32[3,8,9,256,9]{3,4,2,1,0:T(8,128)S(1)} fusion(f32[9,9,1,1,1]{1,0,4,3,2:T(8,128)S(1)} %copy-done.13, f32[3,8,9,256,9]{3,4,2,1,0:T(8,128)S(1)} %fusion.44, f32[8]{0:T(128)S(1)} %copy-done.31, f32[9,9]{1,0:T(8,128)S(1)} %copy-done.17), kind=kOutput, calls=%fused_computation.49 | convolution fusion | flops 54743040 | bytes 3981992 | tf_op jit(solution)/shard_map/ji,peajl->peail/dot_general | solution.py:112
  294.2 3.9 fusion.35
  298.2 5.9 %fusion.32 = f32[3,8,9,9,256]{4,2,0,1,3:T(8,128)S(1)} fusion(f32[3,8,9,256,9]{3,4,2,1,0:T(8,128)S(1)} %fusion.33, f32[8,9,9]{1,0,2:T(8,128)S(1)} %copy-done.22, f32[256]{0:T(256)S(1)} %pad_maximum_fusion.6, f32[3,8,9,1,256]{4,2,0,1,3:T(8,128)S(1)} %maximum_add_fusion.1, f32[3,8,1,9,256]{4,2,0,1,3:T(1,128)S(1)} %get-tuple-element.32, ...), kind=kOutput, calls=%fused_computation.48 | convolution fusion | flops 61212672 | bytes 8408932 | tf_op jit(solution)/shard_map/ji,pejbl->peibl/dot_general | solution.py:112
  307.5 4.4 %collective-permute-done.2 = f32[3,8,1,9,256]{4,2,0,1,3:T(1,128)S(1)} collective-permute-done((f32[3,8,1,9,256]{4,2,0,1,3:T(1,128)S(1)}, f32[3,8,1,9,256]{4,2,0,1,3:T(1,128)S(1)}, u32[]{:S(2)}, u32[]{:S(2)}) %collective-permute-start.2) | collective-permute-done | bytes 221216 | tf_op jit(solution)/shard_map/ppermute | solution.py:48
  316.5 14.7 %all-reduce.1 = (f32[3,256]{1,0:T(4,128)}, f32[3,256]{1,0:T(4,128)}) all-reduce(f32[3,256]{1,0:T(4,128)} %get-tuple-element.8, f32[3,256]{1,0:T(4,128)} %get-tuple-element.7), channel_id=1, replica_groups=mesh['elem'=8,'mode'=4] {'elem'}, use_global_device_ids=true, to_apply=%region_4.5 | all-reduce | flops 1536 | bytes 12288 | tf_op jit(solution)/shard_map/psum | solution.py:126
  332.5 5.0 %multiply_subtract_fusion = (f32[3,8,9,9,256]{4,2,3,1,0:T(8,128)S(1)}, f32[3,8,9,9,256]{4,2,3,1,0:T(8,128)}) fusion(f32[3,256]{1,0:T(4,128)S(1)} %get-tuple-element.14, f32[3,8,9,9,256]{4,2,0,1,3:T(8,128)S(1)} %fusion.25, f32[3,8,9,1,256]{4,2,3,1,0:T(8,128)} %copy-done.7, f32[3,7,9,256]{3,2,0,1:T(8,128)} %copy-done.12, f32[3,1,9,256]{3,2,0,1:T(8,128)} %copy-done.14, ...), kind=kLoop, calls=%fused_computation.72 | loop fusion | flops 2543616 | bytes 7965696 | tf_op jit(solution)/shard_map/sub | solution.py:211
  337.5 4.9 %fusion.39 = f32[3,8,9,256,9]{3,4,2,1,0:T(8,128)S(1)} fusion(f32[9,9,1,1,1]{1,0,4,3,2:T(8,128)S(1)} %copy-done.13, f32[3,8,9,9,256]{4,2,3,1,0:T(8,128)S(1)} %get-tuple-element.25), kind=kOutput, calls=%fused_computation.58 | convolution fusion | flops 53747712 | bytes 3981636 | tf_op jit(solution)/shard_map/ij,peajl->peail/dot_general | solution.py:109
  342.4 3.4 fusion.30
  345.9 4.1 %fusion.28 = f32[3,8,9,256,9]{3,4,2,1,0:T(8,128)S(1)} fusion(f32[9,9,1,1,1]{1,0,4,3,2:T(8,128)S(1)} %copy-done.13, f32[3,8,9,256,9]{3,4,2,1,0:T(8,128)S(1)} %fusion.39, f32[8]{0:T(128)S(1)} %copy-done.32, f32[9,9]{1,0:T(8,128)S(1)} %copy-done.18), kind=kOutput, calls=%fused_computation.42 | convolution fusion | flops 54743040 | bytes 3981992 | tf_op jit(solution)/shard_map/ji,peajl->peail/dot_general | solution.py:112
  350.0 5.2 %fusion.27 = f32[3,8,9,9,256]{4,2,0,1,3:T(8,128)S(1)} fusion(f32[3,8,9,256,9]{3,4,2,1,0:T(8,128)S(1)} %fusion.28, f32[3,8,9,9,256]{4,2,3,1,0:T(8,128)S(1)} %get-tuple-element.25, f32[9,9,1,1,1]{1,0,2,3,4:T(8,128)S(1)} %copy-done.29, f32[3,8,9,9,256]{4,2,3,1,0:T(8,128)S(1)} %fusion.30, f32[256]{0:T(256)S(1)} %copy-done.40, f32[8,9,9]{1,0,2:T(8,128)S(1)} %copy-done.15), kind=kOutput, calls=%fused_computation.41 | convolution fusion | flops 56236032 | bytes 7966564 | tf_op jit(solution)/shard_map/ji,pejbl->peibl/dot_general | solution.py:112
  358.2 2.6 collective-permute-start.5
  360.8 3.0 copy.136
  363.8 4.8 %concatenate.89 = f32[3,648,2,128]{3,2,0,1:T(2,128)} reshape(f32[3,8,9,9,256]{4,0,3,2,1:T(4,128)} %copy.136) | data formatting | bytes 3981312 | tf_op jit(solution)/shard_map/concatenate | solution.py:97
  370.3 5.0 %copy.155 = f32[3,8,9,9,256]{4,0,3,2,1:T(4,128)} copy(f32[3,8,9,9,256]{4,2,3,1,0:T(8,128)} %get-tuple-element.26) | data formatting | bytes 3981312 | tf_op jit(solution)/shard_map/concatenate | solution.py:97
  375.2 4.5 %concatenate.105 = f32[3,648,2,128]{3,2,0,1:T(2,128)} reshape(f32[3,8,9,9,256]{4,0,3,2,1:T(4,128)} %copy.155) | data formatting | bytes 3981312 | tf_op jit(solution)/shard_map/concatenate | solution.py:97
  379.8 2.5 slice_add_fusion.1
  385.7 12.0 %all-reduce = (f32[3,256]{1,0:T(4,128)S(1)}, f32[3,256]{1,0:T(4,128)S(1)}) all-reduce(f32[3,256]{1,0:T(4,128)S(1)} %get-tuple-element.6, f32[3,256]{1,0:T(4,128)S(1)} %get-tuple-element.5), channel_id=1, replica_groups=mesh['elem'=8,'mode'=4] {'elem'}, use_global_device_ids=true, to_apply=%region_8.9 | all-reduce | flops 1536 | bytes 12288 | tf_op jit(solution)/shard_map/psum | solution.py:126
  397.8 3.6 multiply_add_fusion
  (158 shorter events, 37.4 us)
Async XLA Ops:
  0.0 10.6 %copy-start.37 = (f32[9]{0:T(128)S(1)}, f32[9]{0:T(128)}, u32[]{:S(2)}) copy-start(f32[9]{0:T(128)} %constant.72.clone) | copy-start | bytes 112
  0.0 10.7 %copy-start.38 = (f32[8]{0:T(128)S(1)}, f32[8]{0:T(128)}, u32[]{:S(2)}) copy-start(f32[8]{0:T(128)} %param.8) | copy-start | bytes 100
  0.0 10.7 %copy-start.35 = (s32[8]{0:T(128)S(1)}, s32[8]{0:T(128)}, u32[]{:S(2)}) copy-start(s32[8]{0:T(128)} %param.9) | copy-start | bytes 100
  3.6 52.3 %all-to-all-start = ((f32[3,648,2,128]{3,2,0,1:T(2,128)}), f32[3,648,2,128]{3,2,0,1:T(2,128)S(1)}, u32[]{:S(2)}, u32[]{:S(2)}) async-start(f32[3,648,2,128]{3,2,0,1:T(2,128)} %copy.119), calls=%async_computation | async-start | bytes 3981312 | tf_op jit(solution)/shard_map/all_to_all | solution.py:155
  10.7 31.0 %copy-start.16 = (f32[9,9]{1,0:T(8,128)}, f32[9,9]{1,0:T(8,128)S(1)}, u32[]{:S(2)}) copy-start(f32[9,9]{1,0:T(8,128)S(1)} %copy.118) | copy-start | bytes 976
  13.6 65.5 %copy-start.21 = (f32[1536]{0:T(1024)}, f32[1536]{0:T(1024)S(1)}, u32[]{:S(2)}) copy-start(f32[1536]{0:T(1024)S(1)} %fusion.76) | copy-start | bytes 18436
  57.7 3.6 copy-start.11
  89.5 3.5 copy-start.10
  106.3 19.2 %copy-start.13 = (f32[9,9,1,1,1]{1,0,4,3,2:T(8,128)S(1)}, f32[9,9,1,1,1]{1,0,4,3,2:T(8,128)}, u32[]{:S(2)}) copy-start(f32[9,9,1,1,1]{1,0,4,3,2:T(8,128)} %constant.74) | copy-start | bytes 976
  125.6 11.5 %copy-start.2 = (f32[3,162,1536]{2,0,1:T(4,128)S(1)}, f32[3,162,1536]{2,0,1:T(4,128)}, u32[]{:S(2)}) copy-start(f32[3,162,1536]{2,0,1:T(4,128)} %copy.122) | copy-start | bytes 8957956
  125.6 11.5 %copy-start.3 = (f32[2,9,9,1536]{3,1,2,0:T(8,128)S(1)}, f32[2,9,9,1536]{3,1,2,0:T(8,128)}, u32[]{:S(2)}) copy-start(f32[2,9,9,1536]{3,1,2,0:T(8,128)} %copy.127) | copy-start | bytes 2985988
  125.6 11.5 %copy-start.5 = (f32[3,162,1536]{2,0,1:T(4,128)S(1)}, f32[3,162,1536]{2,0,1:T(4,128)}, u32[]{:S(2)}) copy-start(f32[3,162,1536]{2,0,1:T(4,128)} %copy.128) | copy-start | bytes 8957956
  125.6 11.5 %copy-start.30 = (f32[2]{0:T(128)S(1)}, f32[2]{0:T(128)}, u32[]{:S(2)}) copy-start(f32[2]{0:T(128)} %get-tuple-element.62) | copy-start | bytes 28
  151.4 1.9 copy-start.9
  151.8 2.5 copy-start.8
  182.5 73.1 %all-to-all-start.1 = ((f32[3,162,2,512]{1,2,0,3:T(2,128)}), f32[3,162,2,512]{1,2,0,3:T(2,128)}, u32[]{:S(2)}, u32[]{:S(2)}) async-start(f32[3,162,2,512]{1,2,0,3:T(2,128)} %copy.132), calls=%async_computation.1 | async-start | bytes 6291456 | tf_op jit(solution)/shard_map/all_to_all | solution.py:187
  275.5 6.8 %collective-permute-start = (f32[3,8,1,9,256]{4,2,0,1,3:T(1,128)S(1)}, f32[3,8,1,9,256]{4,2,0,1,3:T(1,128)S(1)}, u32[]{:S(2)}, u32[]{:S(2)}) collective-permute-start(f32[3,8,1,9,256]{4,2,0,1,3:T(1,128)S(1)} %get-tuple-element.33), channel_id=1, source_target_pairs={{0,4},{4,8},{8,12},{12,16},{16,20},{20,24},{24,28},{28,0},{1,5},{5... | collective-permute-start | bytes 663560 | tf_op jit(solution)/shard_map/ppermute | solution.py:48
  275.6 6.8 %collective-permute-start.1 = (f32[3,8,1,9,256]{4,2,0,1,3:T(1,128)S(1)}, f32[3,8,1,9,256]{4,2,0,1,3:T(1,128)S(1)}, u32[]{:S(2)}, u32[]{:S(2)}) collective-permute-start(f32[3,8,1,9,256]{4,2,0,1,3:T(1,128)S(1)} %get-tuple-element.34), channel_id=1, source_target_pairs={{4,0},{8,4},{12,8},{16,12},{20,16},{24,20},{28,24},{0,28},{5,1},{9... | collective-permute-start | bytes 663560 | tf_op jit(solution)/shard_map/ppermute | solution.py:49
  278.2 19.9 %copy-start.39 = (f32[256]{0:T(256)}, f32[256]{0:T(256)S(1)}, u32[]{:S(2)}) copy-start(f32[256]{0:T(256)S(1)} %pad_maximum_fusion.6) | copy-start | bytes 3076
  285.0 4.9 %copy-start.17 = (f32[9,9]{1,0:T(8,128)S(1)}, f32[9,9]{1,0:T(8,128)}, u32[]{:S(2)}) copy-start(f32[9,9]{1,0:T(8,128)} %copy-done.16) | copy-start | bytes 976
  285.0 4.9 %copy-start.31 = (f32[8]{0:T(128)S(1)}, f32[8]{0:T(128)}, u32[]{:S(2)}) copy-start(f32[8]{0:T(128)} %get-tuple-element.57) | copy-start | bytes 100
  290.0 4.2 %copy-start.33 = (f32[8]{0:T(128)S(1)}, f32[8]{0:T(128)}, u32[]{:S(2)}) copy-start(f32[8]{0:T(128)} %get-tuple-element.60) | copy-start | bytes 100
  294.1 4.0 copy-start.22
  294.2 4.0 copy-start.28
  298.1 9.1 %copy-start.36 = (f32[9]{0:T(128)S(1)}, f32[9]{0:T(128)}, u32[]{:S(2)}) copy-start(f32[9]{0:T(128)} %or_select_fusion) | copy-start | bytes 112
  304.3 7.6 %collective-permute-start.2 = (f32[3,8,1,9,256]{4,2,0,1,3:T(1,128)S(1)}, f32[3,8,1,9,256]{4,2,0,1,3:T(1,128)S(1)}, u32[]{:S(2)}, u32[]{:S(2)}) collective-permute-start(f32[3,8,1,9,256]{4,2,0,1,3:T(1,128)S(1)} %get-tuple-element.29), channel_id=1, source_target_pairs={{0,4},{4,8},{8,12},{12,16},{16,20},{20,24},{24,28},{28,0},{1,5},{5... | collective-permute-start | bytes 663560 | tf_op jit(solution)/shard_map/ppermute | solution.py:48
  306.1 5.8 %collective-permute-start.3 = (f32[3,8,1,9,256]{4,2,0,1,3:T(1,128)S(1)}, f32[3,8,1,9,256]{4,2,0,1,3:T(1,128)S(1)}, u32[]{:S(2)}, u32[]{:S(2)}) collective-permute-start(f32[3,8,1,9,256]{4,2,0,1,3:T(1,128)S(1)} %get-tuple-element.30), channel_id=1, source_target_pairs={{4,0},{8,4},{12,8},{16,12},{20,16},{24,20},{28,24},{0,28},{5,1},{9... | collective-permute-start | bytes 663560 | tf_op jit(solution)/shard_map/ppermute | solution.py:49
  307.3 6.2 %copy-start.19 = (f32[9,9]{0,1:T(8,128)}, f32[9,9]{0,1:T(8,128)S(1)}, u32[]{:S(2)}) copy-start(f32[9,9]{0,1:T(8,128)S(1)} %multiply_divide_fusion) | copy-start | bytes 976
  313.4 3.1 copy-start.12
  313.4 3.0 copy-start.14
  314.6 1.9 copy-start.7
  332.5 5.0 %copy-start.23 = (f32[3,256]{1,0:T(4,128)}, f32[3,256]{1,0:T(4,128)S(1)}, u32[]{:S(2)}) copy-start(f32[3,256]{1,0:T(4,128)S(1)} %get-tuple-element.14) | copy-start | bytes 9220
  337.5 12.5 %copy-start = (f32[3,8,9,9,256]{4,2,3,1,0:T(8,128)}, f32[3,8,9,9,256]{4,2,3,1,0:T(8,128)S(1)}, u32[]{:S(2)}) copy-start(f32[3,8,9,9,256]{4,2,3,1,0:T(8,128)S(1)} %get-tuple-element.25) | copy-start | bytes 5971972
  337.5 4.9 %copy-start.34 = (f32[8]{0:T(128)S(1)}, f32[8]{0:T(128)}, u32[]{:S(2)}) copy-start(f32[8]{0:T(128)} %get-tuple-element.60) | copy-start | bytes 100
  342.4 3.4 copy-start.18
  342.4 3.4 copy-start.32
  345.8 4.2 %copy-start.15 = (f32[8,9,9]{1,0,2:T(8,128)S(1)}, f32[8,9,9]{1,0,2:T(8,128)}, u32[]{:S(2)}) copy-start(f32[8,9,9]{1,0,2:T(8,128)} %get-tuple-element.52) | copy-start | bytes 7780
  345.8 4.2 %copy-start.29 = (f32[9,9,1,1,1]{1,0,2,3,4:T(8,128)S(1)}, f32[9,9,1,1,1]{1,0,2,3,4:T(8,128)}, u32[]{:S(2)}) copy-start(f32[9,9,1,1,1]{1,0,2,3,4:T(8,128)} %constant.75) | copy-start | bytes 976
  345.9 4.2 %copy-start.40 = (f32[256]{0:T(256)S(1)}, f32[256]{0:T(256)}, u32[]{:S(2)}) copy-start(f32[256]{0:T(256)} %copy-done.39) | copy-start | bytes 3076
  355.3 1.9 copy-start.6
  358.2 21.6 %collective-permute-start.4 = (f32[3,8,1,9,256]{4,2,0,1,3:T(1,128)}, f32[3,8,1,9,256]{4,2,0,1,3:T(1,128)}, u32[]{:S(2)}, u32[]{:S(2)}) collective-permute-start(f32[3,8,1,9,256]{4,2,0,1,3:T(1,128)} %get-tuple-element.23), channel_id=1, source_target_pairs={{0,4},{4,8},{8,12},{12,16},{16,20},{20,24},{24,28},{28,0},{1,5},{5... | collective-permute-start | bytes 663560 | tf_op jit(solution)/shard_map/ppermute | solution.py:48
  358.2 21.6 %collective-permute-start.5 = (f32[3,8,1,9,256]{4,2,0,1,3:T(1,128)}, f32[3,8,1,9,256]{4,2,0,1,3:T(1,128)}, u32[]{:S(2)}, u32[]{:S(2)}) collective-permute-start(f32[3,8,1,9,256]{4,2,0,1,3:T(1,128)} %get-tuple-element.24), channel_id=1, source_target_pairs={{4,0},{8,4},{12,8},{16,12},{20,16},{24,20},{28,24},{0,28},{5,1},{9... | collective-permute-start | bytes 663560 | tf_op jit(solution)/shard_map/ppermute | solution.py:49
  363.8 6.5 %copy-start.24 = (f32[3,256]{1,0:T(4,128)S(1)}, f32[3,256]{1,0:T(4,128)}, u32[]{:S(2)}) copy-start(f32[3,256]{1,0:T(4,128)} %copy-done.23) | copy-start | bytes 9220
  375.2 4.5 %copy-start.25 = (f32[3,256]{1,0:T(4,128)S(1)}, f32[3,256]{1,0:T(4,128)}, u32[]{:S(2)}) copy-start(f32[3,256]{1,0:T(4,128)} %get-tuple-element.13) | copy-start | bytes 9220
  382.3 2.0 copy-start.1
  382.3 2.0 copy-start.20
  384.3 13.4 %copy-start.26 = (f32[3,256]{1,0:T(4,128)S(1)}, f32[3,256]{1,0:T(4,128)}, u32[]{:S(2)}) copy-start(f32[3,256]{1,0:T(4,128)} %get-tuple-element.11) | copy-start | bytes 9220
  384.3 13.4 %copy-start.27 = (f32[3,256]{1,0:T(4,128)S(1)}, f32[3,256]{1,0:T(4,128)}, u32[]{:S(2)}) copy-start(f32[3,256]{1,0:T(4,128)} %get-tuple-element.12) | copy-start | bytes 9220
  (1 other events, 1.5 us)
where the time goes:
time: 409 us; the launch traced here: 404 us
  matrix products  106 us (26%)
  local copies, waits for them, and re-layouts  84.7 us (21%)
  other arithmetic  79.2 us (19%)
  waiting for transfers between devices  71.7 us (18%)
  blocking collectives  39.5 us (10%)
  starting transfers between devices  19.2 us (5%)
    all_to_all x1, waiting for transfers between devices, on_device(): lax.all_to_all(spectral, 'mode', split_axis=3, concat_axis=1, tiled=True)  63.4 us
    psum x2, blocking collectives, paired(): lax.psum((weighted_sum(residual, residual, multiplicity), weighted_sum(re...  26.7 us
    concatenate x4, local copies, waits for them, and re-layouts, assemble(): jnp.concatenate([jnp.roll(upper_layer, 1, axis=1)[:, :, :, None], nodal_f...  17.2 us
    dot_general x1, matrix products, on_device(): jnp.einsum('peabq,ql->peabl', tendency, forward, precision=highest)  17.1 us
    dot_general x1, matrix products, on_device(): jnp.einsum('ij,pejbq->peibq', derivative, values, precision=highest)  14.2 us
    mul x2, other arithmetic, spectral_tables(): -wave_number * mode_weight * sine_table  14.2 us
    mul x1, other arithmetic, spectral_tables(): -mode_weight * sine_table  14.2 us
    cos x1, other arithmetic, spectral_tables(): cosine_table = jnp.cos(angles)  14 us
  transfers between devices with their start and end apart: 8, of which 3 were waited for; matrix products, arithmetic and copies ran while one was open for 17% of the time, Pallas kernels for 0%

commit v1 on v0

v1 whole, which is shorter than its diff:
```python
import math

import jax
import jax.numpy as jnp
import numpy as np
from jax import lax
from jax.experimental import pallas as pl
from jax.experimental.pallas import tpu as pltpu
from jax.sharding import PartitionSpec as P

ORDER = 8
NPT = 9
N2 = 81
PAD = 88
ROWS = 248

gll_points = [
    -1.0,
    -0.8997579954114602,
    -0.6771862795107377,
    -0.3631174638261782,
    0.0,
    0.3631174638261782,
    0.6771862795107377,
    0.8997579954114602,
    1.0,
]
gll_weights = [
    0.0277777777777778,
    0.1654953615608055,
    0.2745387125001617,
    0.3464285109730463,
    0.3715192743764172,
    0.3464285109730463,
    0.2745387125001617,
    0.1654953615608055,
    0.0277777777777778,
]
viscosity = 0.5
time_step = 0.02
thrust_coef = 4.0 / 3.0
f32 = jnp.float32
bf16 = jnp.bfloat16


def derivative_matrix():
    points = np.array(gll_points)
    identity = np.eye(9)
    differences = points[:, None] - points[None, :] + identity
    barycentric = 1.0 / np.prod(differences, axis=1)
    off_diagonal = barycentric[None, :] / barycentric[:, None] / differences * (1.0 - identity)
    return off_diagonal - identity * off_diagonal.sum(axis=1)[:, None]


def split_host(table):
    import ml_dtypes

    high = table.astype(np.float32).astype(ml_dtypes.bfloat16)
    low = (table - high.astype(np.float64)).astype(np.float32).astype(ml_dtypes.bfloat16)
    return jnp.asarray(high), jnp.asarray(low)


def split_xla(table):
    high = lax.reduce_precision(table, 8, 7)
    return high.astype(bf16), (table - high).astype(bf16)


def split(x):
    high = x.astype(bf16)
    return high, (x - high.astype(f32)).astype(bf16)


def dot(a, b):
    return jnp.dot(a, b, preferred_element_type=f32)


def dot_nt(a, b):
    return lax.dot_general(a, b, (((1,), (1,)), ((), ())), preferred_element_type=f32)


def dot3(a, b, d=dot):
    return d(a[0], b[0]) + d(a[0], b[1]) + d(a[1], b[0])


def physical_kernel(
    groups, modes, tile, planes, scale_ref, x_ref, chi, clo, shi, slo, ghi, glo, wk, w2,
    out_ref, xr, xi, rh, rl, ih, il, col0, acc_re, acc_im, press,
):
    q = pl.program_id(0)
    half = planes // 2

    @pl.when(q == 0)
    def _():
        xr[...] = jnp.zeros_like(xr)
        xi[...] = jnp.zeros_like(xi)
        for g in range(groups):
            lanes = slice(g * modes, (g + 1) * modes)
            cw = wk[0:1, lanes]
            ck = wk[1:2, lanes]
            for i in range(3):
                re = x_ref[g, 0, N2 * i : N2 * i + N2, :]
                im = x_ref[g, 1, N2 * i : N2 * i + N2, :]
                at = slice(PAD * i, PAD * i + N2)
                zt = slice(3 * PAD + PAD * i, 3 * PAD + PAD * i + N2)
                xr[at, lanes] = cw * re
                xi[at, lanes] = cw * im
                xr[zt, lanes] = -ck * im
                xi[zt, lanes] = ck * re
        full = xr[...]
        rh[...], rl[...] = split(full)
        ih[...], il[...] = split(xi[...])
        col0[...] = jnp.broadcast_to(
            jnp.sum(full * wk[2:3, :], axis=1, keepdims=True), col0.shape
        )
        acc_re[...] = jnp.zeros_like(acc_re)
        acc_im[...] = jnp.zeros_like(acc_im)
        press[...] = jnp.zeros_like(press)

    ctab = (chi[...], clo[...])
    stab = (shi[...], slo[...])
    cpart = dot3((rh[...], rl[...]), ctab)
    spart = dot3((ih[...], il[...]), stab)
    lane = lax.broadcasted_iota(jnp.int32, (1, tile), 1) + q * tile
    first = lane == 0
    side_a = cpart - spart
    side_b = jnp.where(first, col0[:, 0:1], cpart + spart)
    plane_b = jnp.where(first, half, planes - lane)
    grad = (ghi[...], glo[...])
    tend = []
    total = jnp.zeros((PAD, tile), f32)
    for side, plane in ((side_a, lane), (side_b, plane_b)):
        inside = ((plane >= 3 * planes // 8) & (plane < 5 * planes // 8)).astype(f32)
        u = [side[PAD * i : PAD * i + PAD] for i in range(3)]
        z = [side[3 * PAD + PAD * i : 4 * PAD + PAD * i] for i in range(3)]
        ux = u[0] * scale_ref[0]
        uy = u[1] * scale_ref[1]
        total = total + u[0] * u[0] * inside
        parts = []
        for i in range(3):
            g = dot3(grad, split(u[i]))
            parts.append(-(ux * g[:PAD] + uy * g[PAD:] + u[2] * z[i]))
        tend.append(jnp.concatenate(parts, axis=0))
    press[...] += total * w2[...]
    plus = split(tend[0] + tend[1])
    minus = split(tend[0] - tend[1])
    acc_re[...] += dot3(plus, ctab, dot_nt)
    acc_im[...] -= dot3(minus, stab, dot_nt)

    @pl.when(q == 0)
    def _():
        acc_re[...] += tend[1][:, 0:1] * (wk[2:3, :] - 1.0)

    @pl.when(q == pl.num_programs(0) - 1)
    def _():
        coef = math.sqrt(groups * modes) / planes
        whole = jnp.sum(jnp.sum(press[...], axis=1, keepdims=True), axis=0, keepdims=True)
        tail = jnp.broadcast_to(whole, (ROWS - 3 * N2, modes))
        for g in range(groups):
            lanes = slice(g * modes, (g + 1) * modes)
            for part, acc in ((0, acc_re), (1, acc_im)):
                for i in range(3):
                    out_ref[g, part, N2 * i : N2 * i + N2, :] = (
                        coef * acc[PAD * i : PAD * i + N2, lanes]
                    )
                out_ref[g, part, 3 * N2 : ROWS, :] = tail


def physical(received, scales, tables, grads, wk, w2):
    groups, _, _, modes = received.shape
    count = groups * modes
    planes = 3 * count
    half = planes // 2
    tile = 256 if half % 256 == 0 else half
    table_spec = pl.BlockSpec((count, tile), lambda q: (0, q))
    whole = lambda a: pl.BlockSpec(a.shape, lambda q: (0,) * a.ndim)
    body = lambda *refs: physical_kernel(groups, modes, tile, planes, *refs)
    flops = 3 * 2 * (6 * PAD + 3 * PAD) * count * planes
    return pl.pallas_call(
        body,
        grid=(half // tile,),
        out_shape=jax.ShapeDtypeStruct(received.shape, f32),
        in_specs=[pl.BlockSpec(memory_space=pltpu.SMEM), whole(received)]
        + [table_spec] * 4
        + [whole(grads[0]), whole(grads[1]), whole(wk), whole(w2)],
        out_specs=whole(received),
        scratch_shapes=[
            pltpu.VMEM((6 * PAD, count), f32),
            pltpu.VMEM((6 * PAD, count), f32),
            pltpu.VMEM((6 * PAD, count), bf16),
            pltpu.VMEM((6 * PAD, count), bf16),
            pltpu.VMEM((6 * PAD, count), bf16),
            pltpu.VMEM((6 * PAD, count), bf16),
            pltpu.VMEM((6 * PAD, 128), f32),
            pltpu.VMEM((3 * PAD, count), f32),
            pltpu.VMEM((3 * PAD, count), f32),
            pltpu.VMEM((PAD, tile), f32),
        ],
        cost_estimate=pl.CostEstimate(
            flops=flops, bytes_accessed=8 * count * half, transcendentals=0
        ),
        compiler_params=pltpu.CompilerParams(vmem_limit_bytes=48 << 20),
    )(scales, received, *tables, *grads, wk, w2)


def stiffness_line():
    d = derivative_matrix()
    w = np.array(gll_weights)
    k = d.T @ (w[:, None] * d)
    even = np.zeros((5, 5))
    odd = np.zeros((4, 4))
    for i in range(5):
        for j in range(5):
            even[i, j] = k[i, j] if j == 4 else 0.5 * (k[i, j] + k[i, 8 - j])
    for i in range(4):
        for j in range(4):
            odd[i, j] = 0.5 * (k[i, j] - k[i, 8 - j])
    return even, odd


def line_product(v, even, odd):
    s = [v[j] + v[8 - j] for j in range(4)] + [v[4]]
    t = [v[j] - v[8 - j] for j in range(4)]
    ev = [sum(float(even[i, j]) * s[j] for j in range(5)) for i in range(5)]
    od = [sum(float(odd[i, j]) * t[j] for j in range(4)) for i in range(4)]
    return [ev[i] + od[i] for i in range(4)] + [ev[4]] + [ev[i] - od[i] for i in range(3, -1, -1)]


def cg_kernel(
    chunks, groups, elems, modes, peers,
    mf_ref, rx_ref, ry_ref, jw_ref, cw_ref, th_ref, tk_ref, *refs,
):
    vel = refs[:chunks]
    ret = refs[chunks : 2 * chunks]
    out_ref = refs[2 * chunks]
    (r, qb, from_left, from_right, dots, gathered, coef, fs, fr, ds, dr) = refs[2 * chunks + 1 :]
    me = lax.axis_index("elem")
    face = NPT * elems
    w = gll_weights
    even, odd = stiffness_line()
    mult = [0.5] + [1.0] * 7 + [0.5]

    barrier = pltpu.get_barrier_semaphore()
    for k in range(1, peers):
        pl.semaphore_signal(
            barrier, inc=1, device_id={"elem": lax.rem(me + k, peers)},
            device_id_type=pl.DeviceIdType.MESH,
        )

    pressure = jnp.zeros((1, modes), f32)
    for e in range(elems):
        pressure = pressure + cw_ref[e : e + 1, :] * ret[e % chunks][
            e // chunks, 0, 3 * N2 : 3 * N2 + 1, :
        ]
    for e in range(elems):
        g, c = e // chunks, e % chunks
        for part in range(2):
            push = th_ref[e : e + 1, :] * pressure * tk_ref[part : part + 1, :]
            for i in range(3):
                rows = slice(N2 * i, N2 * i + N2)
                value = vel[c][g, part, rows, :] + time_step * ret[c][g, part, rows, :]
                if i == 0:
                    value = value + push
                r[2 * i + part, pl.ds(e, N2, stride=elems), :] = value

    def row(a, b):
        return pl.ds((a * NPT + b) * elems, elems)

    def joined(line):
        top = line[8] + pltpu.roll(line[0], elems - 1, 0)
        return [pltpu.roll(top, 1, 0)] + line[1:8] + [top]

    def masses(p, carry):
        jw = jw_ref[...]
        for a in range(NPT):
            line = [r[p, row(a, b), :] * (jw * (w[a] * w[b])) for b in range(NPT)]
            line = joined(line)
            for b in range(NPT):
                r[p, row(a, b), :] = line[b]
        return carry

    lax.fori_loop(0, 6, masses, 0)
    pl.semaphore_wait(barrier, peers - 1)

    right, left = lax.rem(me + 1, peers), lax.rem(me + peers - 1, peers)

    def face_copies(buffer, n):
        one = pltpu.make_async_remote_copy(
            src_ref=buffer.at[:, pl.ds(8 * face, face), :],
            dst_ref=from_left.at[n],
            send_sem=fs.at[2 * n],
            recv_sem=fr.at[2 * n],
            device_id={"elem": right},
            device_id_type=pl.DeviceIdType.MESH,
        )
        two = pltpu.make_async_remote_copy(
            src_ref=buffer.at[:, pl.ds(0, face), :],
            dst_ref=from_right.at[n],
            send_sem=fs.at[2 * n + 1],
            recv_sem=fr.at[2 * n + 1],
            device_id={"elem": left},
            device_id_type=pl.DeviceIdType.MESH,
        )
        return one, two

    def dot_copies(n):
        copies = []
        for k in range(1, peers):
            copies.append(
                pltpu.make_async_remote_copy(
                    src_ref=dots.at[n],
                    dst_ref=gathered.at[n, k - 1],
                    send_sem=ds.at[n, k - 1],
                    recv_sem=dr.at[n, k - 1],
                    device_id={"elem": lax.rem(me + k, peers)},
                    device_id_type=pl.DeviceIdType.MESH,
                )
            )
        return copies

    def add_faces(buffer, n):
        buffer[:, pl.ds(0, face), :] = buffer[:, pl.ds(0, face), :] + from_left[n]
        buffer[:, pl.ds(8 * face, face), :] = buffer[:, pl.ds(8 * face, face), :] + from_right[n]

    copies = face_copies(r, 0)
    for c in copies:
        c.start()
    for c in copies:
        c.wait()
    add_faces(r, 0)

    def squash(x):
        return jnp.sum(x, axis=0, keepdims=True)

    def apply_first(p, carry):
        mf, rx, ry = mf_ref[...], rx_ref[...], ry_ref[...]
        for b in range(NPT):
            v = [r[p, row(a, b), :] for a in range(NPT)]
            kx = line_product(v, even, odd)
            rxb = rx * w[b]
            mfb = mf * w[b]
            for a in range(NPT):
                qb[p, row(a, b), :] = (mfb * w[a]) * v[a] + rxb * kx[a]
        rr = jnp.zeros((elems, modes), f32)
        pq = jnp.zeros((elems, modes), f32)
        for a in range(NPT):
            v = [r[p, row(a, b), :] for b in range(NPT)]
            ky = line_product(v, even, odd)
            rya = ry * w[a]
            line = [qb[p, row(a, b), :] + rya * ky[b] for b in range(NPT)]
            for b in range(NPT):
                rr = rr + (mult[a] * mult[b]) * (v[b] * v[b])
                pq = pq + v[b] * line[b]
            line = joined(line)
            for b in range(NPT):
                qb[p, row(a, b), :] = line[b]
        dots[0, pl.ds(p, 1), :] = squash(rr)
        dots[0, pl.ds(8 + p, 1), :] = squash(pq)
        return carry

    dots[...] = jnp.zeros_like(dots)
    lax.fori_loop(0, 6, apply_first, 0)
    faces = face_copies(qb, 1)
    sums = dot_copies(0)
    for c in faces + tuple(sums):
        c.start()
    for c in sums:
        c.wait()
    total = dots[0]
    for k in range(peers - 1):
        total = total + gathered[0, k]
    norm = total[0:8]
    alpha = norm / total[8:16]
    coef[0] = alpha
    for c in faces:
        c.wait()
    add_faces(qb, 1)

    def apply_second(p, carry):
        mf, rx, ry = mf_ref[...], rx_ref[...], ry_ref[...]
        al = coef[0, pl.ds(p, 1), :]
        rz = jnp.zeros((elems, modes), f32)
        rr = jnp.zeros((elems, modes), f32)
        for b in range(NPT):
            v = [r[p, row(a, b), :] - al * qb[p, row(a, b), :] for a in range(NPT)]
            kx = line_product(v, even, odd)
            one = jnp.zeros((elems, modes), f32)
            two = jnp.zeros((elems, modes), f32)
            for a in range(NPT):
                qb[p, row(a, b), :] = v[a]
                square = v[a] * v[a]
                one = one + v[a] * kx[a]
                two = two + w[a] * square
                rr = rr + (mult[a] * mult[b]) * square
            rz = rz + w[b] * (rx * one + mf * two)
        for a in range(NPT):
            v = [qb[p, row(a, b), :] for b in range(NPT)]
            ky = line_product(v, even, odd)
            one = jnp.zeros((elems, modes), f32)
            for b in range(NPT):
                one = one + v[b] * ky[b]
            rz = rz + (w[a] * ry) * one
        dots[1, pl.ds(p, 1), :] = squash(rr)
        dots[1, pl.ds(8 + p, 1), :] = squash(rz)
        return carry

    lax.fori_loop(0, 6, apply_second, 0)
    sums = dot_copies(1)
    for c in sums:
        c.start()
    for c in sums:
        c.wait()
    later = dots[1]
    for k in range(peers - 1):
        later = later + gathered[1, k]
    following = later[0:8]
    beta = following / norm
    second = following / (later[8:16] - beta * following / alpha)
    coef[0] = alpha + second * beta
    coef[1] = second

    def finish(p, carry):
        first = coef[0, pl.ds(p, 1), :]
        last = coef[1, pl.ds(p, 1), :]
        r[p] = first * r[p] + last * qb[p]
        return carry

    lax.fori_loop(0, 6, finish, 0)
    for i in range(3):
        for part in range(2):
            for e in range(elems):
                out_ref[i, part, e * N2 : e * N2 + N2, :] = r[
                    2 * i + part, pl.ds(e, N2, stride=elems), :
                ]


def conjugate_gradients(vels, rets, small):
    chunks = len(vels)
    groups, _, _, modes = vels[0].shape
    elems = groups * chunks
    peers = lax.axis_size("elem")
    body = lambda *refs: cg_kernel(chunks, groups, elems, modes, peers, *refs)
    vm = pl.BlockSpec(memory_space=pltpu.VMEM)
    return pl.pallas_call(
        body,
        out_shape=jax.ShapeDtypeStruct((3, 2, elems * N2, modes), f32),
        in_specs=[vm] * (len(small) + 2 * chunks),
        out_specs=vm,
        scratch_shapes=[
            pltpu.VMEM((6, N2 * elems, modes), f32),
            pltpu.VMEM((6, N2 * elems, modes), f32),
            pltpu.VMEM((2, 6, NPT * elems, modes), f32),
            pltpu.VMEM((2, 6, NPT * elems, modes), f32),
            pltpu.VMEM((2, 16, modes), f32),
            pltpu.VMEM((2, peers - 1, 16, modes), f32),
            pltpu.VMEM((2, 8, modes), f32),
            pltpu.SemaphoreType.DMA((4,)),
            pltpu.SemaphoreType.DMA((4,)),
            pltpu.SemaphoreType.DMA((2, peers - 1)),
            pltpu.SemaphoreType.DMA((2, peers - 1)),
        ],
        compiler_params=pltpu.CompilerParams(
            collective_id=0, has_side_effects=True, vmem_limit_bytes=48 << 20
        ),
    )(*small, *vels, *rets)


def on_device(velocity, column_width, row_height, disc_mask):
    groups = lax.axis_size("mode")
    modes = velocity.shape[3]
    count = groups * modes
    planes = 3 * count
    half = planes // 2
    elems = velocity.shape[1] // N2
    chunks = elems // groups
    mine = lax.axis_index("mode")
    hx = column_width[0]

    shaped = velocity.reshape(3, groups, chunks, N2, 2, modes)
    vels = []
    for c in range(chunks):
        piece = jnp.transpose(shaped[:, :, c], (1, 3, 0, 2, 4)).reshape(groups, 2, 3 * N2, modes)
        vels.append(jnp.pad(piece, ((0, 0), (0, 0), (0, ROWS - 3 * N2), (0, 0))))
    received = [lax.all_to_all(v, "mode", 0, 0, tiled=True) for v in vels]

    k = jnp.arange(count, dtype=jnp.int32)
    j = jnp.arange(half, dtype=jnp.int32)
    phase = k[:, None] * j[None, :] % planes
    angles = 2.0 * math.pi / planes * phase.astype(f32)
    tables = split_xla(jnp.cos(angles)) + split_xla(jnp.sin(angles))

    derivative = derivative_matrix()
    stacked = np.zeros((2 * PAD, PAD))
    stacked[:N2, :N2] = np.kron(derivative, np.eye(9))
    stacked[PAD : PAD + N2, :N2] = np.kron(np.eye(9), derivative)
    grads = split_host(stacked)
    host_k = np.arange(count)
    weight = np.where(host_k == 0, 1.0, 2.0) / math.sqrt(count)
    wk = np.zeros((8, count), np.float32)
    wk[0] = weight
    wk[1] = weight * (8.0 / count) * host_k
    wk[2] = 1.0 - 2.0 * (host_k % 2)
    wk = jnp.asarray(wk)
    w = np.array(gll_weights)
    tile = 256 if half % 256 == 0 else half
    w2 = np.zeros((PAD, 1), np.float32)
    w2[:N2, 0] = (w[:, None] * w[None, :]).reshape(-1)
    w2 = jnp.asarray(np.broadcast_to(w2, (PAD, tile)))

    rets = []
    for c in range(chunks):
        hy = lax.dynamic_index_in_dim(row_height, mine * chunks + c, keepdims=False)
        scales = jnp.stack([2.0 / hx, 2.0 / hy])
        spectral = physical(received[c], scales, tables, grads, wk, w2)
        rets.append(lax.all_to_all(spectral, "mode", 0, 0, tiled=True))

    disc = disc_mask.astype(f32)
    jacobian = hx * row_height / 4.0
    disc_planes = 5 * planes // 8 - 3 * planes // 8
    area = disc_planes * hx * jnp.sum(disc * row_height)
    spread = lambda x: jnp.broadcast_to(x[:, None], (elems, modes))
    local_k = (mine * modes + jnp.arange(modes, dtype=jnp.int32)).astype(f32)
    kz = 8.0 / count * local_k
    factor = 1.0 / time_step + viscosity * kz * kz
    in_planes = np.arange(3 * planes // 8, 5 * planes // 8)
    arg = 2.0 * np.pi * ((host_k[:, None] * in_planes[None, :]) % planes) / planes
    profile = math.sqrt(count) / planes * np.stack([np.cos(arg).sum(1), -np.sin(arg).sum(1)])
    profile = jnp.asarray(profile.astype(np.float32)).reshape(2, groups, modes)
    small = (
        jacobian[:, None] * factor[None, :],
        spread(viscosity * row_height / hx),
        spread(viscosity * hx / row_height),
        spread(jacobian / time_step),
        spread(disc * jacobian),
        spread(-(0.5 * thrust_coef * ORDER * time_step) / hx * disc / area),
        lax.dynamic_index_in_dim(profile, mine, axis=1, keepdims=False),
    )
    result = conjugate_gradients(vels, rets, small)
    result = result.reshape(3, 2, elems * N2, modes)
    return jnp.transpose(result, (0, 2, 1, 3))


def solution(mesh):
    return jax.shard_map(
        on_device,
        mesh=mesh,
        in_specs=(P(None, "elem", None, "mode"), P("elem"), P(), P("elem")),
        out_specs=P(None, "elem", None, "mode"),
        check_vma=False,
    )
```

time: 409 us -> 150 us (0.37); the launches traced: 404 us -> 150 us
  matrix products: 106 us -> 0 us
  local copies, waits for them, and re-layouts: 84.7 us -> 13.2 us
  other arithmetic: 79.2 us -> 14.3 us
  Pallas kernels: 0 us -> 43.4 us
  blocking collectives: 39.5 us -> 0 us
  waiting for transfers between devices: 71.7 us -> 57.5 us
    dot_general x13 -> x0, matrix products: 106 us -> none  [the longest x1 17.1 us: on_device(): jnp.einsum('peabq,ql->peabl', tendency, forward, precision=highest)]
    pallas_call x0 -> x3, Pallas kernels: none -> 43.4 us  [the longest x1 26.2 us: conjugate_gradients(): pl.pallas_call(body, out_shape=jax.ShapeDtypeStruct((3, 2, elems * N2, mo...]
    mul x12 -> x1, other arithmetic: 41.7 us -> 0.07 us  [on_device(): jacobian[:, None] * factor[None, :]]
    psum x3 -> x0, blocking collectives: 39.5 us -> none  [the longest x2 26.7 us: paired(): lax.psum((weighted_sum(residual, residual, multiplicity), weighted_sum(re...]
    mul x14 -> x0, local copies, waits for them, and re-layouts: 22.7 us -> none  [the longest x2 11.1 us: on_device(): time_step * returned.reshape(3, elements, 9, 9, 2 * local_modes)]
    concatenate x8 -> x0, local copies, waits for them, and re-layouts: 17.3 us -> none  [the longest x4 17.2 us: assemble(): jnp.concatenate([jnp.roll(upper_layer, 1, axis=1)[:, :, :, None], nodal_f...]
    reshape x4 -> x2, local copies, waits for them, and re-layouts: 16.5 us -> 0.14 us  [on_device(): jnp.transpose(shaped[:, :, c], (1, 3, 0, 2, 4))]
    cos x1 -> x0, other arithmetic: 14 us -> none  [spectral_tables(): cosine_table = jnp.cos(angles)]
  transfers between devices with their start and end apart: 8 -> 4, of which waited for: 3 -> 3; matrix products, arithmetic and copies ran while one was open for 17% -> 11% of each run, Pallas kernels for 0% -> 12%
where the time goes in v1:
time: 150 us
  waiting for transfers between devices  57.5 us (38%)
  Pallas kernels  43.4 us (29%)
  starting transfers between devices  18.4 us (12%)
  other arithmetic  14.3 us (10%)
  local copies, waits for them, and re-layouts  13.2 us (9%)
  between operations  2.9 us (2%)
    all_to_all x2, waiting for transfers between devices, on_device(): rets.append(lax.all_to_all(spectral, 'mode', 0, 0, tiled=True))  33.7 us
    pallas_call x1, Pallas kernels, conjugate_gradients(): pl.pallas_call(body, out_shape=jax.ShapeDtypeStruct((3, 2, elems * N2, mo...  26.2 us
    all_to_all x2, waiting for transfers between devices, on_device(): received = [lax.all_to_all(v, 'mode', 0, 0, tiled=True) for v in vels]  23.8 us
    pallas_call x2, Pallas kernels, physical(): pl.pallas_call(body, grid=(half // tile,), out_shape=jax.ShapeDtypeStruct...  17.2 us
    convert_element_type x2, other arithmetic, split_xla(): return (high.astype(bf16), (table - high).astype(bf16))  13.4 us
    all_to_all x2, starting transfers between devices, on_device(): received = [lax.all_to_all(v, 'mode', 0, 0, tiled=True) for v in vels]  9.86 us
    all_to_all x2, starting transfers between devices, on_device(): rets.append(lax.all_to_all(spectral, 'mode', 0, 0, tiled=True))  8.57 us
    unnamed x26, local copies, waits for them, and re-layouts  5.33 us
  transfers between devices with their start and end apart: 4, of which 3 were waited for; matrix products, arithmetic and copies ran while one was open for 11% of the time, Pallas kernels for 12%

profile of v1, /device:TPU:0, one launch (start us, length us, event | category | flops | bytes accessed | tf_op | source)
XLA Modules:
  0.0 149.8 jit_solution(17515269877624594893)
XLA Ops:
  0.0 1.6 %fusion.9 = (f32[3,4,1,81,2,128]{5,4,3,2,1,0:T(2,128)S(1)}, f32[3,4,1,81,2,128]{5,4,3,2,1,0:T(2,128)S(1)}) fusion(f32[3,4,2,81,2,128]{5,4,3,2,1,0:T(2,128)} %bitcast.24), kind=kLoop, calls=%fused_computation.27 | loop fusion | bytes 3981312 | tf_op jit(solution)/shard_map/slice | solution.py:481
  1.6 0.1 copy.19
  1.7 0.1 copy.16
  1.8 1.1 pad.8.refs_8_
  2.9 6.3 %all-to-all-start.2 = ((f32[4,2,248,128]{3,2,1,0:T(8,128)}), f32[4,2,248,128]{3,2,1,0:T(8,128)S(1)}, u32[]{:S(2)}, u32[]{:S(2)}) async-start(f32[4,2,248,128]{3,2,1,0:T(8,128)} %pad.8.refs_8_), calls=%async_computation.2 | async-start | bytes 2031616 | tf_op jit(solution)/shard_map/all_to_all | solution.py:483
  9.2 0.1 copy.18
  9.3 0.1 copy.14
  9.3 0.0 copy-start.9
  9.4 1.0 pad.7.refs_7_
  10.4 23.8 %all-to-all-done.2.refs_1_ = f32[4,2,248,128]{3,2,1,0:T(8,128)S(1)} async-done(((f32[4,2,248,128]{3,2,1,0:T(8,128)}), f32[4,2,248,128]{3,2,1,0:T(8,128)S(1)}, u32[]{:S(2)}, u32[]{:S(2)}) %all-to-all-start.2) | async-done | bytes 1015840 | tf_op jit(solution)/shard_map/all_to_all | solution.py:483
  34.2 3.5 %all-to-all-start = ((f32[4,2,248,128]{3,2,1,0:T(8,128)}), f32[4,2,248,128]{3,2,1,0:T(8,128)S(1)}, u32[]{:S(2)}, u32[]{:S(2)}) async-start(f32[4,2,248,128]{3,2,1,0:T(8,128)} %pad.7.refs_7_), calls=%async_computation | async-start | bytes 2031616 | tf_op jit(solution)/shard_map/all_to_all | solution.py:483
  38.4 0.0 copy-done.9
  38.4 0.7 fusion.10
  39.8 0.1 pad_maximum_fusion.1.refs_0_
  39.9 0.0 copy-start.11
  39.9 6.6 %reduce-precision_convert_fusion = (bf16[512,768]{1,0:T(8,128)(2,1)S(1)}, bf16[512,768]{1,0:T(8,128)(2,1)S(1)}) fusion(), kind=kLoop, calls=%fused_computation.2 | loop fusion | flops 5111808 | bytes 1572864 | tf_op jit(solution)/shard_map/convert_element_type | solution.py:65
  46.5 0.0 copy-start
  46.5 6.8 %fusion = (bf16[512,768]{1,0:T(8,128)(2,1)S(1)}, bf16[512,768]{1,0:T(8,128)(2,1)S(1)}) fusion(), kind=kLoop, calls=%fused_computation.5 | loop fusion | flops 5898240 | bytes 1572864 | tf_op jit(solution)/shard_map/convert_element_type | solution.py:65
  53.3 0.0 copy-done.11
  53.3 0.1 jit_solution_.3.refs_9_
  53.4 0.0 copy-done
  53.4 0.0 copy-done.6
  53.4 0.0 copy-done.7
  53.4 0.0 copy-done.8
  53.4 8.6 %shard_map.92 = f32[4,2,248,128]{3,2,1,0:T(8,128)} custom-call(f32[2]{0:T(128)S(1)} %pad_maximum_fusion.1.refs_0_, f32[4,2,248,128]{3,2,1,0:T(8,128)S(1)} %all-to-all-done.2.refs_1_, bf16[512,768]{1,0:T(8,128)(2,1)S(1)} %get-tuple-element.19.refs_2_, bf16[512,768]{1,0:T(8,128)(2,1)S(1)} %get-tuple-element.20.refs_3_, ...), custom_call_target="tpu_custom_call" | custom-call | flops 3737124864 | bytes 3145728 | tf_op jit(solution)/shard_map/pallas_call | solution.py:178
  62.1 0.9 copy-done.2
  63.0 0.9 copy-done.4
  63.8 0.0 all-to-all-done.refs_1_
  63.8 5.1 %all-to-all-start.3 = ((f32[4,2,248,128]{3,2,1,0:T(8,128)}), f32[4,2,248,128]{3,2,1,0:T(8,128)S(1)}, u32[]{:S(2)}, u32[]{:S(2)}) async-start(f32[4,2,248,128]{3,2,1,0:T(8,128)} %shard_map.92), calls=%async_computation.3 | async-start | bytes 2031616 | tf_op jit(solution)/shard_map/all_to_all | solution.py:514
  69.6 0.1 pad_maximum_fusion.refs_0_
  69.7 1.1 copy-done.1
  70.8 1.1 copy-done.3
  71.9 1.1 copy-done.5
  73.1 8.6 %shard_map.91 = f32[4,2,248,128]{3,2,1,0:T(8,128)} custom-call(f32[2]{0:T(128)S(1)} %pad_maximum_fusion.refs_0_, f32[4,2,248,128]{3,2,1,0:T(8,128)S(1)} %all-to-all-done.refs_1_, bf16[512,768]{1,0:T(8,128)(2,1)S(1)} %copy-done.1, bf16[512,768]{1,0:T(8,128)(2,1)S(1)} %copy-done.3, bf16[512,768]{1,0:T(8,128)(2,1)S(1)} %get-tuple-element.18.refs_4_, ...), custom_call_target="tpu_custom_call" | custom-call | flops 3737124864 | bytes 3145728 | tf_op jit(solution)/shard_map/pallas_call | solution.py:178
  81.7 11.3 %all-to-all-done.3.refs_10_ = f32[4,2,248,128]{3,2,1,0:T(8,128)S(1)} async-done(((f32[4,2,248,128]{3,2,1,0:T(8,128)}), f32[4,2,248,128]{3,2,1,0:T(8,128)S(1)}, u32[]{:S(2)}, u32[]{:S(2)}) %all-to-all-start.3) | async-done | bytes 1015840 | tf_op jit(solution)/shard_map/all_to_all | solution.py:514
  92.9 3.5 %all-to-all-start.1 = ((f32[4,2,248,128]{3,2,1,0:T(8,128)}), f32[4,2,248,128]{3,2,1,0:T(8,128)S(1)}, u32[]{:S(2)}, u32[]{:S(2)}) async-start(f32[4,2,248,128]{3,2,1,0:T(8,128)} %shard_map.91), calls=%async_computation.1 | async-start | bytes 2031616 | tf_op jit(solution)/shard_map/all_to_all | solution.py:514
  96.5 0.0 copy-done.10
  96.5 0.7 multiply_multiply_fusion
  97.8 0.7 dynamic-slice_bitcast_fusion.refs_6_
  98.5 0.1 broadcast_multiply_fusion.refs_0_
  98.6 22.4 %all-to-all-done.1.refs_9_ = f32[4,2,248,128]{3,2,1,0:T(8,128)S(1)} async-done(((f32[4,2,248,128]{3,2,1,0:T(8,128)}), f32[4,2,248,128]{3,2,1,0:T(8,128)S(1)}, u32[]{:S(2)}, u32[]{:S(2)}) %all-to-all-start.1) | async-done | bytes 1015840 | tf_op jit(solution)/shard_map/all_to_all | solution.py:514
  121.0 0.1 broadcast_in_dim.14.refs_5_
  121.1 0.1 broadcast_in_dim.10.refs_1_
  121.1 0.1 broadcast_in_dim.11.refs_2_
  121.2 0.1 broadcast_in_dim.12.refs_3_
  121.3 0.1 broadcast_in_dim.13.refs_4_
  121.4 26.2 %shard_map.93 = f32[3,2,648,128]{3,2,1,0:T(8,128)S(1)} custom-call(f32[8,128]{1,0:T(8,128)S(1)} %broadcast_multiply_fusion.refs_0_, f32[8,128]{1,0:T(8,128)S(1)} %broadcast_in_dim.10.refs_1_, f32[8,128]{1,0:T(8,128)S(1)} %broadcast_in_dim.11.refs_2_, f32[8,128]{1,0:T(8,128)S(1)} %broadcast_in_dim.12.refs_3_, f32[8,128]{1,0:T(8,128)S(1)} %broadcast_in_dim.13.refs_4_, ...), custom_call_target="tpu_custom_call" | custom-call | tf_op jit(solution)/shard_map/pallas_call | solution.py:443
  147.5 2.3 %copy.17 = f32[3,648,2,128]{3,2,1,0:T(2,128)} copy(f32[3,648,2,128]{3,1,2,0:T(8,128)S(1)} %bitcast.21) | data formatting | bytes 3981312 | tf_op jit(solution)/shard_map/transpose | solution.py:539
  (11 shorter events, 0.0 us)
Async XLA Ops:
  2.9 31.4 %all-to-all-start.2 = ((f32[4,2,248,128]{3,2,1,0:T(8,128)}), f32[4,2,248,128]{3,2,1,0:T(8,128)S(1)}, u32[]{:S(2)}, u32[]{:S(2)}) async-start(f32[4,2,248,128]{3,2,1,0:T(8,128)} %pad.8.refs_8_), calls=%async_computation.2 | async-start | bytes 2031616 | tf_op jit(solution)/shard_map/all_to_all | solution.py:483
  9.3 29.1 %copy-start.9 = (f32[8]{0:T(128)S(1)}, f32[8]{0:T(128)}, u32[]{:S(2)}) copy-start(f32[8]{0:T(128)} %param.11) | copy-start | bytes 100
  34.2 29.6 %all-to-all-start = ((f32[4,2,248,128]{3,2,1,0:T(8,128)}), f32[4,2,248,128]{3,2,1,0:T(8,128)S(1)}, u32[]{:S(2)}, u32[]{:S(2)}) async-start(f32[4,2,248,128]{3,2,1,0:T(8,128)} %pad.7.refs_7_), calls=%async_computation | async-start | bytes 2031616 | tf_op jit(solution)/shard_map/all_to_all | solution.py:483
  39.9 13.5 %copy-start.11 = (f32[88]{0:T(128)S(1)}, f32[88]{0:T(128)}, u32[]{:S(2)}) copy-start(f32[88]{0:T(128)} %constant.81.clone) | copy-start | bytes 1060
  39.9 13.6 %copy-start.6 = (bf16[176,88]{1,0:T(8,128)(2,1)S(1)}, bf16[176,88]{1,0:T(8,128)(2,1)}, u32[]{:S(2)}) copy-start(bf16[176,88]{1,0:T(8,128)(2,1)} %constant.78.clone.refs_6_) | copy-start | bytes 92932
  39.9 13.6 %copy-start.7 = (bf16[176,88]{1,0:T(8,128)(2,1)S(1)}, bf16[176,88]{1,0:T(8,128)(2,1)}, u32[]{:S(2)}) copy-start(bf16[176,88]{1,0:T(8,128)(2,1)} %constant.79.clone.refs_7_) | copy-start | bytes 92932
  39.9 13.6 %copy-start.8 = (f32[8,512]{1,0:T(8,128)S(1)}, f32[8,512]{1,0:T(8,128)}, u32[]{:S(2)}) copy-start(f32[8,512]{1,0:T(8,128)} %constant.80.clone.refs_8_) | copy-start | bytes 49156
  46.5 6.9 %copy-start = (bf16[512,768]{1,0:T(8,128)(2,1)}, bf16[512,768]{1,0:T(8,128)(2,1)S(1)}, u32[]{:S(2)}) copy-start(bf16[512,768]{1,0:T(8,128)(2,1)S(1)} %get-tuple-element.19.refs_2_) | copy-start | bytes 2359300
  62.1 0.9 copy-start.2
  63.0 0.9 copy-start.4
  63.8 29.1 %all-to-all-start.3 = ((f32[4,2,248,128]{3,2,1,0:T(8,128)}), f32[4,2,248,128]{3,2,1,0:T(8,128)S(1)}, u32[]{:S(2)}, u32[]{:S(2)}) async-start(f32[4,2,248,128]{3,2,1,0:T(8,128)} %shard_map.92), calls=%async_computation.3 | async-start | bytes 2031616 | tf_op jit(solution)/shard_map/all_to_all | solution.py:514
  69.7 1.1 copy-start.1
  70.8 1.1 copy-start.3
  71.9 1.1 copy-start.5
  81.7 14.8 %copy-start.10 = (s32[8]{0:T(128)S(1)}, s32[8]{0:T(128)}, u32[]{:S(2)}) copy-start(s32[8]{0:T(128)} %param.12) | copy-start | bytes 100
  92.9 28.1 %all-to-all-start.1 = ((f32[4,2,248,128]{3,2,1,0:T(8,128)}), f32[4,2,248,128]{3,2,1,0:T(8,128)S(1)}, u32[]{:S(2)}, u32[]{:S(2)}) async-start(f32[4,2,248,128]{3,2,1,0:T(8,128)} %shard_map.91), calls=%async_computation.1 | async-start | bytes 2031616 | tf_op jit(solution)/shard_map/all_to_all | solution.py:514

commit v2 on v1

--- a/solution.py
+++ b/solution.py
@@ -60,11 +60,6 @@
     return jnp.asarray(high), jnp.asarray(low)
 
 
-def split_xla(table):
-    high = lax.reduce_precision(table, 8, 7)
-    return high.astype(bf16), (table - high).astype(bf16)
-
-
 def split(x):
     high = x.astype(bf16)
     return high, (x - high.astype(f32)).astype(bf16)
@@ -82,124 +77,87 @@
     return d(a[0], b[0]) + d(a[0], b[1]) + d(a[1], b[0])
 
 
-def physical_kernel(
-    groups, modes, tile, planes, scale_ref, x_ref, chi, clo, shi, slo, ghi, glo, wk, w2,
-    out_ref, xr, xi, rh, rl, ih, il, col0, acc_re, acc_im, press,
-):
-    q = pl.program_id(0)
+def advect_chunk(groups, modes, tile, planes, scales, x, spec, small, tabs, scratch):
+    ghi, glo, wk, w2 = small
+    ch, cl, sh, sl = tabs
+    xr, xi, rh, rl, ih, il, col0, acc_re, acc_im, press = scratch
     half = planes // 2
-
-    @pl.when(q == 0)
-    def _():
-        xr[...] = jnp.zeros_like(xr)
-        xi[...] = jnp.zeros_like(xi)
-        for g in range(groups):
-            lanes = slice(g * modes, (g + 1) * modes)
-            cw = wk[0:1, lanes]
-            ck = wk[1:2, lanes]
+    for g in range(groups):
+        lanes = slice(g * modes, (g + 1) * modes)
+        cw = wk[0:1, lanes]
+        ck = wk[1:2, lanes]
+        for i in range(3):
+            re = x[g, 0, N2 * i : N2 * i + N2, :]
+            im = x[g, 1, N2 * i : N2 * i + N2, :]
+            at = slice(PAD * i, PAD * i + N2)
+            zt = slice(3 * PAD + PAD * i, 3 * PAD + PAD * i + N2)
+            xr[at, lanes] = cw * re
+            xi[at, lanes] = cw * im
+            xr[zt, lanes] = -ck * im
+            xi[zt, lanes] = ck * re
+    full = xr[...]
+    rh[...], rl[...] = split(full)
+    ih[...], il[...] = split(xi[...])
+    col0[...] = jnp.broadcast_to(jnp.sum(full * wk[2:3, :], axis=1, keepdims=True), col0.shape)
+    acc_re[...] = jnp.zeros_like(acc_re)
+    acc_im[...] = jnp.zeros_like(acc_im)
+    press[...] = jnp.zeros_like(press)
+
+    def step(q, carry):
+        ctab = (ch[q], cl[q])
+        stab = (sh[q], sl[q])
+        cpart = dot3((rh[...], rl[...]), ctab)
+        spart = dot3((ih[...], il[...]), stab)
+        lane = lax.broadcasted_iota(jnp.int32, (1, tile), 1) + q * tile
+        first = lane == 0
+        side_a = cpart - spart
+        side_b = jnp.where(first, col0[:, 0:1], cpart + spart)
+        plane_b = jnp.where(first, half, planes - lane)
+        grad = (ghi[...], glo[...])
+        tend = []
+        total = jnp.zeros((PAD, tile), f32)
+        for side, plane in ((side_a, lane), (side_b, plane_b)):
+            inside = ((plane >= 3 * planes // 8) & (plane < 5 * planes // 8)).astype(f32)
+            u = [side[PAD * i : PAD * i + PAD] for i in range(3)]
+            z = [side[3 * PAD + PAD * i : 4 * PAD + PAD * i] for i in range(3)]
+            ux = u[0] * scales[0]
+            uy = u[1] * scales[1]
+            total = total + u[0] * u[0] * inside
+            parts = []
             for i in range(3):
-                re = x_ref[g, 0, N2 * i : N2 * i + N2, :]
-                im = x_ref[g, 1, N2 * i : N2 * i + N2, :]
-                at = slice(PAD * i, PAD * i + N2)
-                zt = slice(3 * PAD + PAD * i, 3 * PAD + PAD * i + N2)
-                xr[at, lanes] = cw * re
-                xi[at, lanes] = cw * im
-                xr[zt, lanes] = -ck * im
-                xi[zt, lanes] = ck * re
-        full = xr[...]
-        rh[...], rl[...] = split(full)
-        ih[...], il[...] = split(xi[...])
-        col0[...] = jnp.broadcast_to(
-            jnp.sum(full * wk[2:3, :], axis=1, keepdims=True), col0.shape
-        )
-        acc_re[...] = jnp.zeros_like(acc_re)
-        acc_im[...] = jnp.zeros_like(acc_im)
-        press[...] = jnp.zeros_like(press)
-
-    ctab = (chi[...], clo[...])
-    stab = (shi[...], slo[...])
-    cpart = dot3((rh[...], rl[...]), ctab)
-    spart = dot3((ih[...], il[...]), stab)
-    lane = lax.broadcasted_iota(jnp.int32, (1, tile), 1) + q * tile
-    first = lane == 0
-    side_a = cpart - spart
-    side_b = jnp.where(first, col0[:, 0:1], cpart + spart)
-    plane_b = jnp.where(first, half, planes - lane)
-    grad = (ghi[...], glo[...])
-    tend = []
-    total = jnp.zeros((PAD, tile), f32)
-    for side, plane in ((side_a, lane), (side_b, plane_b)):
-        inside = ((plane >= 3 * planes // 8) & (plane < 5 * planes // 8)).astype(f32)
-        u = [side[PAD * i : PAD * i + PAD] for i in range(3)]
-        z = [side[3 * PAD + PAD * i : 4 * PAD + PAD * i] for i in range(3)]
-        ux = u[0] * scale_ref[0]
-        uy = u[1] * scale_ref[1]
-        total = total + u[0] * u[0] * inside
-        parts = []
-        for i in range(3):
-            g = dot3(grad, split(u[i]))
-            parts.append(-(ux * g[:PAD] + uy * g[PAD:] + u[2] * z[i]))
-        tend.append(jnp.concatenate(parts, axis=0))
-    press[...] += total * w2[...]
-    plus = split(tend[0] + tend[1])
-    minus = split(tend[0] - tend[1])
-    acc_re[...] += dot3(plus, ctab, dot_nt)
-    acc_im[...] -= dot3(minus, stab, dot_nt)
-
-    @pl.when(q == 0)
-    def _():
-        acc_re[...] += tend[1][:, 0:1] * (wk[2:3, :] - 1.0)
-
-    @pl.when(q == pl.num_programs(0) - 1)
-    def _():
-        coef = math.sqrt(groups * modes) / planes
-        whole = jnp.sum(jnp.sum(press[...], axis=1, keepdims=True), axis=0, keepdims=True)
-        tail = jnp.broadcast_to(whole, (ROWS - 3 * N2, modes))
-        for g in range(groups):
-            lanes = slice(g * modes, (g + 1) * modes)
-            for part, acc in ((0, acc_re), (1, acc_im)):
-                for i in range(3):
-                    out_ref[g, part, N2 * i : N2 * i + N2, :] = (
-                        coef * acc[PAD * i : PAD * i + N2, lanes]
-                    )
-                out_ref[g, part, 3 * N2 : ROWS, :] = tail
-
-
-def physical(received, scales, tables, grads, wk, w2):
-    groups, _, _, modes = received.shape
-    count = groups * modes
-    planes = 3 * count
-    half = planes // 2
-    tile = 256 if half % 256 == 0 else half
-    table_spec = pl.BlockSpec((count, tile), lambda q: (0, q))
-    whole = lambda a: pl.BlockSpec(a.shape, lambda q: (0,) * a.ndim)
-    body = lambda *refs: physical_kernel(groups, modes, tile, planes, *refs)
-    flops = 3 * 2 * (6 * PAD + 3 * PAD) * count * planes
-    return pl.pallas_call(
-        body,
-        grid=(half // tile,),
-        out_shape=jax.ShapeDtypeStruct(received.shape, f32),
-        in_specs=[pl.BlockSpec(memory_space=pltpu.SMEM), whole(received)]
-        + [table_spec] * 4
-        + [whole(grads[0]), whole(grads[1]), whole(wk), whole(w2)],
-        out_specs=whole(received),
-        scratch_shapes=[
-            pltpu.VMEM((6 * PAD, count), f32),
-            pltpu.VMEM((6 * PAD, count), f32),
-            pltpu.VMEM((6 * PAD, count), bf16),
-            pltpu.VMEM((6 * PAD, count), bf16),
-            pltpu.VMEM((6 * PAD, count), bf16),
-            pltpu.VMEM((6 * PAD, count), bf16),
-            pltpu.VMEM((6 * PAD, 128), f32),
-            pltpu.VMEM((3 * PAD, count), f32),
-            pltpu.VMEM((3 * PAD, count), f32),
-            pltpu.VMEM((PAD, tile), f32),
-        ],
-        cost_estimate=pl.CostEstimate(
-            flops=flops, bytes_accessed=8 * count * half, transcendentals=0
-        ),
-        compiler_params=pltpu.CompilerParams(vmem_limit_bytes=48 << 20),
-    )(scales, received, *tables, *grads, wk, w2)
+                g = dot3(grad, split(u[i]))
+                parts.append(-(ux * g[:PAD] + uy * g[PAD:] + u[2] * z[i]))
+            tend.append(jnp.concatenate(parts, axis=0))
+        press[...] += total * w2[...]
+        plus = split(tend[0] + tend[1])
+        minus = split(tend[0] - tend[1])
+        acc_re[...] += dot3(plus, ctab, dot_nt)
+        acc_im[...] -= dot3(minus, stab, dot_nt)
+
+        @pl.when(q == 0)
+        def _():
+            acc_re[...] += tend[1][:, 0:1] * (wk[2:3, :] - 1.0)
+
+        return carry
+
+    lax.fori_loop(0, half // tile, step, 0)
+    coef = math.sqrt(groups * modes) / planes
+    whole = jnp.sum(jnp.sum(press[...], axis=1, keepdims=True), axis=0, keepdims=True)
+    tail = jnp.broadcast_to(whole, (ROWS - 3 * N2, modes))
+    for g in range(groups):
+        lanes = slice(g * modes, (g + 1) * modes)
+        for part, acc in ((0, acc_re), (1, acc_im)):
+            for i in range(3):
+                spec[g, part, N2 * i : N2 * i + N2, :] = (
+                    coef * acc[PAD * i : PAD * i + N2, lanes]
+                )
+            spec[g, part, 3 * N2 : ROWS, :] = tail
+
+
+def partners(me, groups):
+    if groups == 4:
+        return [lax.rem(me + 2, 4), 3 - me, me + 1 - 2 * lax.rem(me, 2)]
+    return [lax.rem(me + k, groups) for k in range(1, groups)]
 
 
 def stiffness_line():
@@ -225,19 +183,25 @@
     return [ev[i] + od[i] for i in range(4)] + [ev[4]] + [ev[i] - od[i] for i in range(3, -1, -1)]
 
 
-def cg_kernel(
-    chunks, groups, elems, modes, peers,
-    mf_ref, rx_ref, ry_ref, jw_ref, cw_ref, th_ref, tk_ref, *refs,
+def window_kernel(
+    chunks, groups, elems, modes, peers, tile,
+    scale_ref, mf_ref, rx_ref, ry_ref, jw_ref, cw_ref, th_ref, tk_ref,
+    cbase, sbase, rot, ghi, glo, wk, w2, *refs,
 ):
     vel = refs[:chunks]
-    ret = refs[chunks : 2 * chunks]
-    out_ref = refs[2 * chunks]
-    (r, qb, from_left, from_right, dots, gathered, coef, fs, fr, ds, dr) = refs[2 * chunks + 1 :]
+    out_ref = refs[chunks]
+    (
+        r, qb, from_left, from_right, dots, gathered, coef, fs, fr, ds, dr,
+        recv, spec, ret, ch, cl, sh, sl, ms, mr, *scratch,
+    ) = refs[chunks + 1 :]
     me = lax.axis_index("elem")
+    slot = lax.axis_index("mode")
+    planes = 3 * groups * modes
     face = NPT * elems
     w = gll_weights
     even, odd = stiffness_line()
     mult = [0.5] + [1.0] * 7 + [0.5]
+    others = partners(slot, groups)
 
     barrier = pltpu.get_barrier_semaphore()
     for k in range(1, peers):
@@ -245,22 +209,70 @@
             barrier, inc=1, device_id={"elem": lax.rem(me + k, peers)},
             device_id_type=pl.DeviceIdType.MESH,
         )
-
+    for other in others:
+        pl.semaphore_signal(
+            barrier, inc=1, device_id={"mode": other}, device_id_type=pl.DeviceIdType.MESH
+        )
+    pl.semaphore_wait(barrier, peers - 1 + groups - 1)
+
+    def exchange(source, target, n):
+        return [
+            pltpu.make_async_remote_copy(
+                src_ref=source.at[other],
+                dst_ref=target.at[slot],
+                send_sem=ms.at[n, k],
+                recv_sem=mr.at[n, k],
+                device_id={"mode": other},
+                device_id_type=pl.DeviceIdType.MESH,
+            )
+            for k, other in enumerate(others)
+        ]
+
+    outward = [exchange(vel[c], recv.at[c], c) for c in range(chunks)]
+    for copies in outward:
+        for copy in copies:
+            copy.start()
+    for c in range(chunks):
+        recv[c, slot] = vel[c][slot]
+    xr, xi = scratch[0], scratch[1]
+    xr[...] = jnp.zeros_like(xr)
+    xi[...] = jnp.zeros_like(xi)
+    cos0, sin0 = cbase[...], sbase[...]
+    for q in range(planes // 2 // tile):
+        cq, sq = rot[:, 2 * q : 2 * q + 1], rot[:, 2 * q + 1 : 2 * q + 2]
+        ch[q], cl[q] = split(cos0 * cq - sin0 * sq)
+        sh[q], sl[q] = split(sin0 * cq + cos0 * sq)
+
+    inward = []
+    for c in range(chunks):
+        for copy in outward[c]:
+            copy.wait()
+        scales = (scale_ref[c, 0], scale_ref[c, 1])
+        advect_chunk(
+            groups, modes, tile, planes, scales, recv.at[c], spec.at[c],
+            (ghi, glo, wk, w2), (ch, cl, sh, sl), scratch,
+        )
+        copies = exchange(spec.at[c], ret.at[c], chunks + c)
+        for copy in copies:
+            copy.start()
+        ret[c, slot] = spec[c, slot]
+        inward.append(copies)
+
+    for c in range(chunks):
+        for copy in inward[c]:
+            copy.wait()
+        for g in range(groups):
+            for part in range(2):
+                for i in range(3):
+                    rows = slice(N2 * i, N2 * i + N2)
+                    value = vel[c][g, part, rows, :] + time_step * ret[c, g, part, rows, :]
+                    r[2 * i + part, pl.ds(g * chunks + c, N2, stride=elems), :] = value
     pressure = jnp.zeros((1, modes), f32)
     for e in range(elems):
-        pressure = pressure + cw_ref[e : e + 1, :] * ret[e % chunks][
-            e // chunks, 0, 3 * N2 : 3 * N2 + 1, :
+        pressure = pressure + cw_ref[e : e + 1, :] * ret[
+            e % chunks, e // chunks, 0, 3 * N2 : 3 * N2 + 1, :
         ]
-    for e in range(elems):
-        g, c = e // chunks, e % chunks
-        for part in range(2):
-            push = th_ref[e : e + 1, :] * pressure * tk_ref[part : part + 1, :]
-            for i in range(3):
-                rows = slice(N2 * i, N2 * i + N2)
-                value = vel[c][g, part, rows, :] + time_step * ret[c][g, part, rows, :]
-                if i == 0:
-                    value = value + push
-                r[2 * i + part, pl.ds(e, N2, stride=elems), :] = value
+    push_all = th_ref[...] * pressure
 
     def row(a, b):
         return pl.ds((a * NPT + b) * elems, elems)
@@ -271,15 +283,15 @@
 
     def masses(p, carry):
         jw = jw_ref[...]
+        push = push_all * tk_ref[pl.ds(p, 1), :]
         for a in range(NPT):
-            line = [r[p, row(a, b), :] * (jw * (w[a] * w[b])) for b in range(NPT)]
+            line = [(r[p, row(a, b), :] + push) * (jw * (w[a] * w[b])) for b in range(NPT)]
             line = joined(line)
             for b in range(NPT):
                 r[p, row(a, b), :] = line[b]
         return carry
 
     lax.fori_loop(0, 6, masses, 0)
-    pl.semaphore_wait(barrier, peers - 1)
 
     right, left = lax.rem(me + 1, peers), lax.rem(me + peers - 1, peers)
 
@@ -433,17 +445,23 @@
                 ]
 
 
-def conjugate_gradients(vels, rets, small):
+def window(vels, scales, small, tables):
     chunks = len(vels)
     groups, _, _, modes = vels[0].shape
     elems = groups * chunks
+    count = groups * modes
+    half = 3 * count // 2
+    tile = tables[0].shape[1]
     peers = lax.axis_size("elem")
-    body = lambda *refs: cg_kernel(chunks, groups, elems, modes, peers, *refs)
+    body = lambda *refs: window_kernel(chunks, groups, elems, modes, peers, tile, *refs)
     vm = pl.BlockSpec(memory_space=pltpu.VMEM)
+    block = (chunks, groups, 2, ROWS, modes)
+    table = pltpu.VMEM((half // tile, count, tile), bf16)
     return pl.pallas_call(
         body,
         out_shape=jax.ShapeDtypeStruct((3, 2, elems * N2, modes), f32),
-        in_specs=[vm] * (len(small) + 2 * chunks),
+        in_specs=[pl.BlockSpec(memory_space=pltpu.SMEM)]
+        + [vm] * (len(small) + len(tables) + chunks),
         out_specs=vm,
         scratch_shapes=[
             pltpu.VMEM((6, N2 * elems, modes), f32),
@@ -457,11 +475,30 @@
             pltpu.SemaphoreType.DMA((4,)),
             pltpu.SemaphoreType.DMA((2, peers - 1)),
             pltpu.SemaphoreType.DMA((2, peers - 1)),
+            pltpu.VMEM(block, f32),
+            pltpu.VMEM(block, f32),
+            pltpu.VMEM(block, f32),
+            table,
+            table,
+            table,
+            table,
+            pltpu.SemaphoreType.DMA((2 * chunks, groups - 1)),
+            pltpu.SemaphoreType.DMA((2 * chunks, groups - 1)),
+            pltpu.VMEM((6 * PAD, count), f32),
+            pltpu.VMEM((6 * PAD, count), f32),
+            pltpu.VMEM((6 * PAD, count), bf16),
+            pltpu.VMEM((6 * PAD, count), bf16),
+            pltpu.VMEM((6 * PAD, count), bf16),
+            pltpu.VMEM((6 * PAD, count), bf16),
+            pltpu.VMEM((6 * PAD, 128), f32),
+            pltpu.VMEM((3 * PAD, count), f32),
+            pltpu.VMEM((3 * PAD, count), f32),
+            pltpu.VMEM((PAD, tile), f32),
         ],
         compiler_params=pltpu.CompilerParams(
-            collective_id=0, has_side_effects=True, vmem_limit_bytes=48 << 20
+            collective_id=0, has_side_effects=True, vmem_limit_bytes=56 << 20
         ),
-    )(*small, *vels, *rets)
+    )(scales, *small, *tables, *vels)
 
 
 def on_device(velocity, column_width, row_height, disc_mask):
@@ -480,14 +517,6 @@
     for c in range(chunks):
         piece = jnp.transpose(shaped[:, :, c], (1, 3, 0, 2, 4)).reshape(groups, 2, 3 * N2, modes)
         vels.append(jnp.pad(piece, ((0, 0), (0, 0), (0, ROWS - 3 * N2), (0, 0))))
-    received = [lax.all_to_all(v, "mode", 0, 0, tiled=True) for v in vels]
-
-    k = jnp.arange(count, dtype=jnp.int32)
-    j = jnp.arange(half, dtype=jnp.int32)
-    phase = k[:, None] * j[None, :] % planes
-    angles = 2.0 * math.pi / planes * phase.astype(f32)
-    tables = split_xla(jnp.cos(angles)) + split_xla(jnp.sin(angles))
-
     derivative = derivative_matrix()
     stacked = np.zeros((2 * PAD, PAD))
     stacked[:N2, :N2] = np.kron(derivative, np.eye(9))
@@ -506,12 +535,14 @@
     w2[:N2, 0] = (w[:, None] * w[None, :]).reshape(-1)
     w2 = jnp.asarray(np.broadcast_to(w2, (PAD, tile)))
 
-    rets = []
-    for c in range(chunks):
-        hy = lax.dynamic_index_in_dim(row_height, mine * chunks + c, keepdims=False)
-        scales = jnp.stack([2.0 / hx, 2.0 / hy])
-        spectral = physical(received[c], scales, tables, grads, wk, w2)
-        rets.append(lax.all_to_all(spectral, "mode", 0, 0, tiled=True))
+    turn = 2.0 * np.pi / planes
+    base = turn * (host_k[:, None] * np.arange(tile)[None, :] % planes)
+    steps = turn * (host_k[:, None] * tile * np.arange(half // tile)[None, :] % planes)
+    rotation = np.stack([np.cos(steps), np.sin(steps)], axis=2).reshape(count, -1)
+    tables = tuple(jnp.asarray(t.astype(np.float32)) for t in (np.cos(base), np.sin(base), rotation))
+    tables = tables + grads + (wk, w2)
+    heights = lax.dynamic_slice_in_dim(row_height, mine * chunks, chunks)
+    scales = jnp.stack([jnp.broadcast_to(2.0 / hx, (chunks,)), 2.0 / heights], axis=1)
 
     disc = disc_mask.astype(f32)
     jacobian = hx * row_height / 4.0
@@ -524,7 +555,8 @@
     in_planes = np.arange(3 * planes // 8, 5 * planes // 8)
     arg = 2.0 * np.pi * ((host_k[:, None] * in_planes[None, :]) % planes) / planes
     profile = math.sqrt(count) / planes * np.stack([np.cos(arg).sum(1), -np.sin(arg).sum(1)])
-    profile = jnp.asarray(profile.astype(np.float32)).reshape(2, groups, modes)
+    profile = np.concatenate([profile, np.zeros((6, count))])
+    profile = jnp.asarray(profile.astype(np.float32)).reshape(8, groups, modes)
     small = (
         jacobian[:, None] * factor[None, :],
         spread(viscosity * row_height / hx),
@@ -534,7 +566,7 @@
         spread(-(0.5 * thrust_coef * ORDER * time_step) / hx * disc / area),
         lax.dynamic_index_in_dim(profile, mine, axis=1, keepdims=False),
     )
-    result = conjugate_gradients(vels, rets, small)
+    result = window(vels, scales, small, tables)
     result = result.reshape(3, 2, elems * N2, modes)
     return jnp.transpose(result, (0, 2, 1, 3))
 

time: 150 us -> 137 us (0.913)
  the two profiles are of different devices: /device:TPU:0 before, /device:TPU:9 now
where the time goes in v2:
time: 137 us
  Pallas kernels  118 us (86%)
  local copies, waits for them, and re-layouts  13.9 us (10%)
  other arithmetic  3.33 us (2%)
    pallas_call x1, Pallas kernels, window(): pl.pallas_call(body, out_shape=jax.ShapeDtypeStruct((3, 2, elems * N2, mo...  118 us
    transpose x1, local copies, waits for them, and re-layouts, on_device(): return jnp.transpose(result, (0, 2, 1, 3))  3.86 us
    broadcast_in_dim x5, local copies, waits for them, and re-layouts, on_device(): spread = lambda x: jnp.broadcast_to(x[:, None], (elems, modes))  3.29 us

profile of v2, /device:TPU:9, one launch (start us, length us, event | category | flops | bytes accessed | tf_op | source)
XLA Modules:
  0.0 136.7 jit_solution(14622145912637959258)
XLA Ops:
  0.7 0.7 divide_bitcast_fusion
  1.5 0.1 copy.17
  1.6 0.7 stack.7.refs_0_
  2.2 1.3 multiply_multiply_fusion
  4.1 0.7 multiply_divide_fusion
  4.7 0.7 broadcast_in_dim.12.refs_4_
  5.4 0.7 broadcast_multiply_fusion.refs_1_
  6.1 0.7 broadcast_in_dim.14.refs_6_
  6.7 1.3 dynamic-slice_bitcast_fusion.refs_7_
  8.0 0.7 broadcast_in_dim.10.refs_2_
  8.6 0.7 broadcast_in_dim.13.refs_5_
  9.3 0.7 broadcast_in_dim.11.refs_3_
  9.9 1.6 %fusion = (f32[3,4,1,81,2,128]{5,4,3,2,1,0:T(2,128)S(1)}, f32[3,4,1,81,2,128]{5,4,3,2,1,0:T(2,128)S(1)}) fusion(f32[3,4,2,81,2,128]{5,4,3,2,1,0:T(2,128)} %bitcast.25), kind=kLoop, calls=%fused_computation.11 | loop fusion | bytes 3981312 | tf_op jit(solution)/shard_map/slice | solution.py:518
  11.6 0.1 copy.24
  11.7 0.1 copy.21
  11.7 1.0 pad.9.refs_16_
  12.8 0.1 copy.23
  12.9 0.0 copy-start
  12.9 0.1 copy.19
  12.9 1.0 pad.8.refs_15_
  14.0 0.0 copy-done
  14.0 0.7 jit_solution_.3.refs_14_
  14.7 118.1 %shard_map.118 = f32[3,2,648,128]{3,2,1,0:T(8,128)} custom-call(f32[2,2]{1,0:T(2,128)} %stack.7.refs_0_, f32[8,128]{1,0:T(8,128)} %broadcast_multiply_fusion.refs_1_, f32[8,128]{1,0:T(8,128)} %broadcast_in_dim.10.refs_2_, f32[8,128]{1,0:T(8,128)} %broadcast_in_dim.11.refs_3_, f32[8,128]{1,0:T(8,128)} %broadcast_in_dim.12.refs_4_, ...), custom_call_target="tpu_custom_call" | custom-call | tf_op jit(solution)/shard_map/pallas_call | solution.py:460
  132.8 3.9 %copy.22 = f32[3,648,2,128]{3,2,1,0:T(2,128)} copy(f32[3,648,2,128]{3,1,2,0:T(8,128)} %bitcast.22) | data formatting | bytes 3981312 | tf_op jit(solution)/shard_map/transpose | solution.py:571
  (1 shorter events, 0.0 us)
Async XLA Ops:
  12.9 1.1 copy-start

commit v3 on v2

--- a/solution.py
+++ b/solution.py
@@ -185,14 +185,13 @@
 
 def window_kernel(
     chunks, groups, elems, modes, peers, tile,
-    scale_ref, mf_ref, rx_ref, ry_ref, jw_ref, cw_ref, th_ref, tk_ref,
-    cbase, sbase, rot, ghi, glo, wk, w2, *refs,
+    hx_ref, hy_ref, disc_ref, tk_ref, cbase, sbase, rot, ghi, glo, wk, w2, *refs,
 ):
     vel = refs[:chunks]
     out_ref = refs[chunks]
     (
         r, qb, from_left, from_right, dots, gathered, coef, fs, fr, ds, dr,
-        recv, spec, ret, ch, cl, sh, sl, ms, mr, *scratch,
+        recv, spec, ret, ch, cl, sh, sl, ms, mr, mf_ref, rx_ref, ry_ref, jw_ref, cw_ref, th_ref, *scratch,
     ) = refs[chunks + 1 :]
     me = lax.axis_index("elem")
     slot = lax.axis_index("mode")
@@ -243,11 +242,31 @@
         ch[q], cl[q] = split(cos0 * cq - sin0 * sq)
         sh[q], sl[q] = split(sin0 * cq + cos0 * sq)
 
+    shape = (elems, modes)
+    for e in range(elems):
+        mf_ref[e : e + 1, :] = jnp.full((1, modes), hy_ref[e], f32)
+        cw_ref[e : e + 1, :] = jnp.full((1, modes), disc_ref[e], jnp.int32).astype(f32)
+    hx, hy, disc = jnp.full(shape, hx_ref[0], f32), mf_ref[...], cw_ref[...]
+    index = slot * modes + lax.broadcasted_iota(jnp.int32, shape, 1)
+    kz = 8.0 / (groups * modes) * index.astype(f32)
+    jacobian = hx * hy / 4.0
+    disc_planes = 5 * planes // 8 - 3 * planes // 8
+    area = disc_planes * hx * jnp.sum(disc * hy, axis=0, keepdims=True)
+    mf_ref[...] = jacobian * (1.0 / time_step + viscosity * kz * kz)
+    rx_ref[...] = viscosity * hy / hx
+    ry_ref[...] = viscosity * hx / hy
+    jw_ref[...] = jacobian / time_step
+    cw_ref[...] = disc * jacobian
+    th_ref[...] = -(0.5 * thrust_coef * ORDER * time_step) / hx * disc / area
+
     inward = []
     for c in range(chunks):
         for copy in outward[c]:
             copy.wait()
-        scales = (scale_ref[c, 0], scale_ref[c, 1])
+        scales = (
+            2.0 / jnp.full((1, tile), hx_ref[0], f32),
+            2.0 / jnp.full((1, tile), hy_ref[slot * chunks + c], f32),
+        )
         advect_chunk(
             groups, modes, tile, planes, scales, recv.at[c], spec.at[c],
             (ghi, glo, wk, w2), (ch, cl, sh, sl), scratch,
@@ -283,7 +302,7 @@
 
     def masses(p, carry):
         jw = jw_ref[...]
-        push = push_all * tk_ref[pl.ds(p, 1), :]
+        push = push_all * tk_ref[slot, pl.ds(p, 1), :]
         for a in range(NPT):
             line = [(r[p, row(a, b), :] + push) * (jw * (w[a] * w[b])) for b in range(NPT)]
             line = joined(line)
@@ -445,13 +464,13 @@
                 ]
 
 
-def window(vels, scales, small, tables):
+def window(vels, scalars, tables):
     chunks = len(vels)
     groups, _, _, modes = vels[0].shape
     elems = groups * chunks
     count = groups * modes
     half = 3 * count // 2
-    tile = tables[0].shape[1]
+    tile = tables[1].shape[1]
     peers = lax.axis_size("elem")
     body = lambda *refs: window_kernel(chunks, groups, elems, modes, peers, tile, *refs)
     vm = pl.BlockSpec(memory_space=pltpu.VMEM)
@@ -460,8 +479,8 @@
     return pl.pallas_call(
         body,
         out_shape=jax.ShapeDtypeStruct((3, 2, elems * N2, modes), f32),
-        in_specs=[pl.BlockSpec(memory_space=pltpu.SMEM)]
-        + [vm] * (len(small) + len(tables) + chunks),
+        in_specs=[pl.BlockSpec(memory_space=pltpu.SMEM)] * len(scalars)
+        + [vm] * (len(tables) + chunks),
         out_specs=vm,
         scratch_shapes=[
             pltpu.VMEM((6, N2 * elems, modes), f32),
@@ -475,7 +494,7 @@
             pltpu.SemaphoreType.DMA((4,)),
             pltpu.SemaphoreType.DMA((2, peers - 1)),
             pltpu.SemaphoreType.DMA((2, peers - 1)),
-            pltpu.VMEM(block, f32),
+            pltpu.VMEM((chunks, groups, 2, 3 * N2, modes), f32),
             pltpu.VMEM(block, f32),
             pltpu.VMEM(block, f32),
             table,
@@ -484,6 +503,9 @@
             table,
             pltpu.SemaphoreType.DMA((2 * chunks, groups - 1)),
             pltpu.SemaphoreType.DMA((2 * chunks, groups - 1)),
+        ]
+        + [pltpu.VMEM((elems, modes), f32)] * 6
+        + [
             pltpu.VMEM((6 * PAD, count), f32),
             pltpu.VMEM((6 * PAD, count), f32),
             pltpu.VMEM((6 * PAD, count), bf16),
@@ -498,7 +520,7 @@
         compiler_params=pltpu.CompilerParams(
             collective_id=0, has_side_effects=True, vmem_limit_bytes=56 << 20
         ),
-    )(scales, *small, *tables, *vels)
+    )(*scalars, *tables, *vels)
 
 
 def on_device(velocity, column_width, row_height, disc_mask):
@@ -509,14 +531,12 @@
     half = planes // 2
     elems = velocity.shape[1] // N2
     chunks = elems // groups
-    mine = lax.axis_index("mode")
-    hx = column_width[0]
 
     shaped = velocity.reshape(3, groups, chunks, N2, 2, modes)
     vels = []
     for c in range(chunks):
         piece = jnp.transpose(shaped[:, :, c], (1, 3, 0, 2, 4)).reshape(groups, 2, 3 * N2, modes)
-        vels.append(jnp.pad(piece, ((0, 0), (0, 0), (0, ROWS - 3 * N2), (0, 0))))
+        vels.append(piece)
     derivative = derivative_matrix()
     stacked = np.zeros((2 * PAD, PAD))
     stacked[:N2, :N2] = np.kron(derivative, np.eye(9))
@@ -533,7 +553,7 @@
     tile = 256 if half % 256 == 0 else half
     w2 = np.zeros((PAD, 1), np.float32)
     w2[:N2, 0] = (w[:, None] * w[None, :]).reshape(-1)
-    w2 = jnp.asarray(np.broadcast_to(w2, (PAD, tile)))
+    w2 = jnp.asarray(w2)
 
     turn = 2.0 * np.pi / planes
     base = turn * (host_k[:, None] * np.arange(tile)[None, :] % planes)
@@ -541,32 +561,13 @@
     rotation = np.stack([np.cos(steps), np.sin(steps)], axis=2).reshape(count, -1)
     tables = tuple(jnp.asarray(t.astype(np.float32)) for t in (np.cos(base), np.sin(base), rotation))
     tables = tables + grads + (wk, w2)
-    heights = lax.dynamic_slice_in_dim(row_height, mine * chunks, chunks)
-    scales = jnp.stack([jnp.broadcast_to(2.0 / hx, (chunks,)), 2.0 / heights], axis=1)
-
-    disc = disc_mask.astype(f32)
-    jacobian = hx * row_height / 4.0
-    disc_planes = 5 * planes // 8 - 3 * planes // 8
-    area = disc_planes * hx * jnp.sum(disc * row_height)
-    spread = lambda x: jnp.broadcast_to(x[:, None], (elems, modes))
-    local_k = (mine * modes + jnp.arange(modes, dtype=jnp.int32)).astype(f32)
-    kz = 8.0 / count * local_k
-    factor = 1.0 / time_step + viscosity * kz * kz
     in_planes = np.arange(3 * planes // 8, 5 * planes // 8)
     arg = 2.0 * np.pi * ((host_k[:, None] * in_planes[None, :]) % planes) / planes
     profile = math.sqrt(count) / planes * np.stack([np.cos(arg).sum(1), -np.sin(arg).sum(1)])
     profile = np.concatenate([profile, np.zeros((6, count))])
-    profile = jnp.asarray(profile.astype(np.float32)).reshape(8, groups, modes)
-    small = (
-        jacobian[:, None] * factor[None, :],
-        spread(viscosity * row_height / hx),
-        spread(viscosity * hx / row_height),
-        spread(jacobian / time_step),
-        spread(disc * jacobian),
-        spread(-(0.5 * thrust_coef * ORDER * time_step) / hx * disc / area),
-        lax.dynamic_index_in_dim(profile, mine, axis=1, keepdims=False),
-    )
-    result = window(vels, scales, small, tables)
+    profile = profile.astype(np.float32).reshape(8, groups, modes).transpose(1, 0, 2)
+    tables = (jnp.asarray(profile),) + tables
+    result = window(vels, (column_width, row_height, disc_mask), tables)
     result = result.reshape(3, 2, elems * N2, modes)
     return jnp.transpose(result, (0, 2, 1, 3))
 

time: 137 us -> 126 us (0.920)
  local copies, waits for them, and re-layouts: 13.9 us -> 7.71 us
  other arithmetic: 3.33 us -> 0 us
    broadcast_in_dim x5 -> x0, local copies, waits for them, and re-layouts: 3.29 us -> none  [on_device(): spread = lambda x: jnp.broadcast_to(x[:, None], (elems, modes))]
    pad x2 -> x0, local copies, waits for them, and re-layouts: 2.06 us -> none  [on_device(): vels.append(jnp.pad(piece, ((0, 0), (0, 0), (0, ROWS - 3 * N2), (0, 0))))]
    div x2 -> x0, other arithmetic: 1.94 us -> none  [the longest x1 1.27 us: on_device(): jacobian / time_step]
    reshape x2, local copies, waits for them, and re-layouts: 0.14 us -> 2.06 us  [on_device(): jnp.transpose(shaped[:, :, c], (1, 3, 0, 2, 4))]
    another operation x3 -> x0, local copies, waits for them, and re-layouts: 1.47 us -> none  [the longest x2 0.75 us: on_device(): jnp.stack([jnp.broadcast_to(2.0 / hx, (chunks,)), 2.0 / heights], axis=1)]
where the time goes in v3:
time: 126 us
  Pallas kernels  117 us (93%)
  local copies, waits for them, and re-layouts  7.71 us (6%)
    pallas_call x1, Pallas kernels, window(): pl.pallas_call(body, out_shape=jax.ShapeDtypeStruct((3, 2, elems * N2, mo...  117 us
    transpose x1, local copies, waits for them, and re-layouts, on_device(): return jnp.transpose(result, (0, 2, 1, 3))  3.86 us

profile of v3, /device:TPU:9, one launch (start us, length us, event | category | flops | bytes accessed | tf_op | source)
XLA Modules:
  0.0 125.6 jit_solution(16085198996582178182)
XLA Ops:
  0.7 1.6 %fusion = (f32[3,4,1,81,2,128]{5,4,3,2,1,0:T(2,128)S(1)}, f32[3,4,1,81,2,128]{5,4,3,2,1,0:T(2,128)S(1)}) fusion(f32[3,4,2,81,2,128]{5,4,3,2,1,0:T(2,128)} %bitcast.15), kind=kLoop, calls=%fused_computation | loop fusion | bytes 3981312 | tf_op jit(solution)/shard_map/slice | solution.py:538
  2.3 0.1 copy.22
  2.4 1.0 copy.19.refs_12_
  3.4 0.1 copy.21
  3.5 1.0 copy.18.refs_11_
  4.5 117.2 %shard_map.118 = f32[3,2,648,128]{3,2,1,0:T(8,128)} custom-call(f32[1]{0:T(128)S(6)} %copy.23.refs_0_, f32[8]{0:T(128)} %refs_1_.1, s32[8]{0:T(128)} %refs_2_.1, f32[4,8,128]{2,1,0:T(8,128)} %constant.23.clone.refs_3_, f32[512,256]{1,0:T(8,128)} %constant.20.clone.refs_4_, f32[512,256]{1,0:T(8,128)} %constant.21.clone.refs_5_, ...), custom_call_target="tpu_custom_call" | custom-call | tf_op jit(solution)/shard_map/pallas_call | solution.py:479
  121.8 3.9 %copy.20 = f32[3,648,2,128]{3,2,1,0:T(2,128)} copy(f32[3,648,2,128]{3,1,2,0:T(8,128)} %bitcast.12) | data formatting | bytes 3981312 | tf_op jit(solution)/shard_map/transpose | solution.py:572
